TPU v7x, 256 devices: a whole 4x4x8 slice. The times are simulated.
256 devices in a mesh: dp: 16 (over y_hi, z), ctx: 16 (over y_lo, x, core).
Axes of the slice: x: 4, y: 4 (y_hi: 2, y_lo: 2; y = y_hi * 2 + y_lo), z: 8, core: 2. Of those that a mesh axis runs over, the one named last changes fastest.
Arguments:
- embeds: bfloat16 [16, 2048, 4096], P('dp', 'ctx'), may hold values from -6 to 6
- norm_gain: float32 [4096], replicated, may hold values from 0.1 to 1.9
- w_key: bfloat16 [4096, 512], P('dp'), may hold values from -0.09375 to 0.09375
- w_value: bfloat16 [4096, 512], P('dp'), may hold values from -0.09375 to 0.09375
- queries: bfloat16 [16, 2048, 4096], P('dp', 'ctx'), may hold values from -85 to 85
- d_out: bfloat16 [16, 2048, 4096], P('dp', 'ctx'), may hold values from -6 to 6
- block_doc: int32 [16, 16], P('dp'), may hold values from 0 to 3, never falling along the last dimension, each value on 1 to 8 neighbouring positions
- slot_order: int32 [16, 32], P('dp'), may hold values from 0 to 31, each once within a row
Outputs:
- grad_embed: bfloat16 [16, 2048, 4096], P('dp', 'ctx')
Inputs may be any that keep to these rules, and one draw needn't show every extreme that they name: `block_doc`: along the blocks of a sequence the document number never falls; each of the 4 documents covers 1 to 8 blocks, and one covers exactly 8. `slot_order`: each row holds every number from 0 to 31 once.
All inputs are finite; a program needn't handle non-finite values.
Results may differ from a plain program's by a relative error of at most 0.035.
The roundings to bfloat16 on the way count: a program that leaves them out, or rounds other values in their place, can miss the bound.
Values may be sent and summed in bfloat16 or wider, within the bound.
No kernel may reach another device: no remote copies, remote signals or barrier semaphores. Data moves between devices by JAX's collectives and lax.ppermute only.
A program may use at most 192 MiB of HBM per device.

v0:
```python
import jax
import jax.numpy as jnp
from jax import lax
from jax.sharding import PartitionSpec as P

HEADS = 32
KV_HEADS = 4
HEAD = 128
DOC_BLOCK = 128


def attend(query_group, dout_group, key_group, value_group, allowed, block_width, score_scale):
    tok_rows, group_size, head_size = query_group.shape
    seq_len = key_group.shape[0]
    block_count = seq_len // block_width
    mask_blocks = allowed.reshape(tok_rows, block_count, block_width)
    live_blocks = jnp.any(mask_blocks, axis=(0, 2))
    mask_blocks = mask_blocks.transpose(1, 0, 2)
    key_blocks = key_group.reshape(block_count, block_width, head_size)
    value_blocks = value_group.reshape(block_count, block_width, head_size)

    def score_block(block_item):
        is_live, key_block, mask_block = block_item
        raw_scores = jnp.einsum(
            "thd,kd->htk", query_group, key_block, preferred_element_type=jnp.float32
        )
        return jnp.where(mask_block[None], raw_scores * score_scale, -jnp.inf)

    scores = lax.map(score_block, (live_blocks, key_blocks, mask_blocks))
    row_max = jnp.max(scores, axis=(0, 3))
    raised = jnp.exp(scores - row_max[None, :, :, None])
    soft_probs = raised / jnp.sum(raised, axis=(0, 3))[None, :, :, None]
    probs_half = soft_probs.astype(jnp.bfloat16)

    def output_block(block_item):
        is_live, prob_half, value_block = block_item
        return jnp.einsum("htk,kd->htd", prob_half, value_block, preferred_element_type=jnp.float32)

    attn_out = jnp.sum(lax.map(output_block, (live_blocks, probs_half, value_blocks)), axis=0)
    row_delta = jnp.einsum("htd,thd->ht", attn_out, dout_group.astype(jnp.float32))

    def grad_block(block_item):
        is_live, prob_block, prob_half, key_block, value_block = block_item
        dprobs = jnp.einsum(
            "thd,kd->htk", dout_group, value_block, preferred_element_type=jnp.float32
        )
        score_grad = (prob_block * (dprobs - row_delta[..., None]) * score_scale).astype(
            jnp.bfloat16
        )
        key_grad = jnp.einsum(
            "htk,thd->kd", score_grad, query_group, preferred_element_type=jnp.float32
        )
        value_grad = jnp.einsum(
            "htk,thd->kd", prob_half, dout_group, preferred_element_type=jnp.float32
        )
        return (key_grad, value_grad)

    key_grad, value_grad = lax.map(
        grad_block, (live_blocks, soft_probs, probs_half, key_blocks, value_blocks)
    )
    return (key_grad.reshape(seq_len, head_size), value_grad.reshape(seq_len, head_size))


def body(embeds, norm_gain, w_key, w_value, queries, d_out, block_doc, slot_order):
    embed_rows = embeds[0]
    tok_rows = embed_rows.shape[0]
    ctx_ways = lax.axis_size("ctx")
    seq_len = tok_rows * ctx_ways
    half_len = tok_rows // 2
    kv_width = KV_HEADS * HEAD
    group_size = HEADS // KV_HEADS
    score_scale = HEAD ** (-0.5)
    as_float = embed_rows.astype(jnp.float32)
    inv_rms = lax.rsqrt(jnp.mean(as_float * as_float, axis=-1, keepdims=True) + 1e-05)
    normed = (as_float * inv_rms * norm_gain).astype(jnp.bfloat16)
    pieces = (
        lax.all_gather(w_key, "dp", axis=0, tiled=True),
        lax.all_gather(w_value, "dp", axis=0, tiled=True),
    )
    key_proj = jnp.dot(normed, pieces[0], preferred_element_type=jnp.float32)
    value_proj = jnp.dot(normed, pieces[1], preferred_element_type=jnp.float32)
    local_kv = jnp.concatenate([key_proj, value_proj], axis=1).astype(jnp.bfloat16)
    all_kv = lax.all_gather(local_kv, "ctx", axis=0, tiled=True)
    row_ids = jnp.arange(seq_len, dtype=jnp.int32)
    slot_hit = (row_ids // half_len)[:, None] == jnp.arange(2 * ctx_ways, dtype=jnp.int32)[None, :]
    key_pos = (
        jnp.sum(jnp.where(slot_hit, slot_order[0][None, :], 0), axis=1) * half_len
        + row_ids % half_len
    )
    block_hit = (key_pos // DOC_BLOCK)[:, None] == jnp.arange(block_doc.shape[1], dtype=jnp.int32)[
        None, :
    ]
    key_doc = jnp.sum(jnp.where(block_hit, block_doc[0][None, :], 0), axis=1)
    row_start = lax.axis_index("ctx") * tok_rows
    query_pos = lax.dynamic_slice_in_dim(key_pos, row_start, tok_rows)
    query_doc = lax.dynamic_slice_in_dim(key_doc, row_start, tok_rows)
    allowed = (key_pos[None, :] <= query_pos[:, None]) & (key_doc[None, :] == query_doc[:, None])
    key_grads = []
    value_grads = []
    for kv_head in range(KV_HEADS):
        first_col = kv_head * group_size * HEAD
        last_col = (kv_head + 1) * group_size * HEAD
        query_group = queries[0][:, first_col:last_col].reshape(tok_rows, group_size, HEAD)
        dout_group = d_out[0][:, first_col:last_col].reshape(tok_rows, group_size, HEAD)
        key_group = all_kv[:, kv_head * HEAD : (kv_head + 1) * HEAD]
        value_group = all_kv[:, kv_width + kv_head * HEAD : kv_width + (kv_head + 1) * HEAD]
        key_grad, value_grad = attend(
            query_group, dout_group, key_group, value_group, allowed, seq_len, score_scale
        )
        key_grads.append(key_grad)
        value_grads.append(value_grad)
    grad_terms = jnp.concatenate(key_grads + value_grads, axis=1)
    own_sum = lax.psum_scatter(
        grad_terms.astype(jnp.bfloat16), "ctx", scatter_dimension=0, tiled=True
    )
    key_half = own_sum[:, :kv_width]
    value_half = own_sum[:, kv_width:]
    contract = (((1,), (1,)), ((), ()))
    pieces = lax.all_gather((w_key, w_value), "dp", axis=0, tiled=True)
    grad_normed = lax.dot_general(
        key_half, pieces[0], contract, preferred_element_type=jnp.float32
    ) + lax.dot_general(value_half, pieces[1], contract, preferred_element_type=jnp.float32)
    mean_term = jnp.mean(as_float * norm_gain * grad_normed, axis=-1, keepdims=True)
    grad_embed = (
        inv_rms * norm_gain * grad_normed - as_float * inv_rms * inv_rms * inv_rms * mean_term
    )
    return grad_embed.astype(jnp.bfloat16)[None]


def solution(mesh):
    in_specs = (
        P("dp", "ctx", None),
        P(),
        P("dp", None),
        P("dp", None),
        P("dp", "ctx", None),
        P("dp", "ctx", None),
        P("dp", None),
        P("dp", None),
    )
    out_specs = P("dp", "ctx", None)
    return jax.shard_map(body, mesh=mesh, in_specs=in_specs, out_specs=out_specs, check_vma=False)
```

profile of v0, /device:TPU:1, one launch (start us, length us, event | category | flops | bytes accessed | tf_op | source)
XLA Modules:
  0.0 442.7 jit_solution(5156086972663562600)
XLA Ops:
  8.1 1.5 fusion.59
  9.6 100.3 %all-gather.6.cloned.1.call-done = bf16[4096,512]{1,0:T(8,128)(2,1)} async-done(((bf16[256,512]{1,0:T(8,128)(2,1)}), bf16[4096,512]{1,0:T(8,128)(2,1)}) %all-gather.6.cloned.1.call-update) | async-done | bytes 4194320 | tf_op jit(solution)/shard_map/all_gather | solution.py:78
  109.9 3.3 convolution_convert_fusion
  113.3 95.6 %all-gather.4.cloned.1.call-done = bf16[4096,512]{1,0:T(8,128)(2,1)} async-done(((bf16[256,512]{1,0:T(8,128)(2,1)}), bf16[4096,512]{1,0:T(8,128)(2,1)}) %all-gather.4.cloned.1.call-update) | async-done | bytes 4194320 | tf_op jit(solution)/shard_map/all_gather | solution.py:77
  208.9 2.9 convolution_convert_fusion.1
  213.7 1.6 copy.87
  217.8 35.1 %all-gather.8.cloned.1.call-done = bf16[2048,1024]{1,0:T(8,128)(2,1)} async-done(((bf16[128,1024]{1,0:T(8,128)(2,1)}), bf16[2048,1024]{1,0:T(8,128)(2,1)}) %all-gather.8.cloned.1.call-update) | async-done | bytes 4194320 | tf_op jit(solution)/shard_map/all_gather | solution.py:83
  253.0 6.9 %fusion.109 = (f32[8,128]{1,0:T(8,128)S(1)}, f32[8,128,2048]{1,2,0:T(8,128)}) fusion(pred[128,2048]{0,1:T(8,128)(4,1)S(1)} %compare_and_fusion, bf16[128,8,128]{0,2,1:T(8,128)(2,1)} %bitcast.281, bf16[2048,1024]{1,0:T(8,128)(2,1)} %all-gather.8.cloned.1.call-done), kind=kOutput, calls=%fused_computation.162 | convolution fusion | flops 545261568 | bytes 9441280 | tf_op jit(solution)/shard_map/sub | solution.py:31
  259.9 6.0 %fusion.33 = bf16[8,128,2048]{1,2,0:T(8,128)(2,1)} fusion(f32[8,128,2048]{1,2,0:T(8,128)} %get-tuple-element.174, f32[8,128]{1,0:T(8,128)S(1)} %get-tuple-element.173), kind=kLoop, calls=%fused_computation.50 | loop fusion | flops 4194304 | bytes 12587008 | tf_op jit(solution)/shard_map/convert_element_type | solution.py:33
  265.9 6.8 %fusion.108 = (f32[8,128]{1,0:T(8,128)S(1)}, f32[8,128,2048]{1,2,0:T(8,128)}) fusion(pred[128,2048]{0,1:T(8,128)(4,1)S(1)} %compare_and_fusion, bf16[128,8,128]{0,2,1:T(8,128)(2,1)S(1)} %bitcast.283, bf16[2048,1024]{1,0:T(8,128)(2,1)} %all-gather.8.cloned.1.call-done), kind=kOutput, calls=%fused_computation.161 | convolution fusion | flops 545261568 | bytes 9441280 | tf_op jit(solution)/shard_map/sub | solution.py:31
  272.8 6.0 %fusion.32 = bf16[8,128,2048]{1,2,0:T(8,128)(2,1)} fusion(f32[8,128,2048]{1,2,0:T(8,128)} %get-tuple-element.172, f32[8,128]{1,0:T(8,128)S(1)} %get-tuple-element.167), kind=kLoop, calls=%fused_computation.49 | loop fusion | flops 4194304 | bytes 12587008 | tf_op jit(solution)/shard_map/convert_element_type | solution.py:33
  278.8 6.8 %fusion.110 = (f32[8,128]{1,0:T(8,128)S(1)}, f32[8,128,2048]{1,2,0:T(8,128)}) fusion(pred[128,2048]{0,1:T(8,128)(4,1)S(1)} %compare_and_fusion, bf16[128,8,128]{0,2,1:T(8,128)(2,1)S(1)} %bitcast.279, bf16[2048,1024]{1,0:T(8,128)(2,1)} %all-gather.8.cloned.1.call-done), kind=kOutput, calls=%fused_computation.163 | convolution fusion | flops 545261568 | bytes 9441280 | tf_op jit(solution)/shard_map/sub | solution.py:31
  285.6 6.0 %fusion.34 = bf16[8,128,2048]{1,2,0:T(8,128)(2,1)} fusion(f32[8,128,2048]{1,2,0:T(8,128)} %get-tuple-element.180, f32[8,128]{1,0:T(8,128)S(1)} %get-tuple-element.175), kind=kLoop, calls=%fused_computation.51 | loop fusion | flops 4194304 | bytes 12587008 | tf_op jit(solution)/shard_map/convert_element_type | solution.py:33
  291.7 7.0 %fusion.111 = (f32[8,128]{1,0:T(8,128)S(1)}, f32[8,128,2048]{1,2,0:T(8,128)}) fusion(pred[128,2048]{0,1:T(8,128)(4,1)S(1)} %compare_and_fusion, bf16[128,8,128]{0,2,1:T(8,128)(2,1)S(1)} %bitcast.277, bf16[2048,1024]{1,0:T(8,128)(2,1)} %all-gather.8.cloned.1.call-done), kind=kOutput, calls=%fused_computation.164 | convolution fusion | flops 545261568 | bytes 9441280 | tf_op jit(solution)/shard_map/sub | solution.py:31
  298.7 6.3 %fusion.35 = bf16[8,128,2048]{1,2,0:T(8,128)(2,1)} fusion(f32[8,128,2048]{1,2,0:T(8,128)} %get-tuple-element.182, f32[8,128]{1,0:T(8,128)S(1)} %get-tuple-element.181), kind=kLoop, calls=%fused_computation.52 | loop fusion | flops 4194304 | bytes 12587008 | tf_op jit(solution)/shard_map/convert_element_type | solution.py:33
  305.0 2.0 fusion.63
  307.3 1.8 fusion.62
  309.2 7.4 %fusion.39 = bf16[2048,1024]{0,1:T(8,128)(2,1)} fusion(bf16[128,8,128]{0,2,1:T(8,128)(2,1)S(1)} %bitcast.284, bf16[128,8,128]{0,2,1:T(8,128)(2,1)S(1)} %bitcast.275, f32[8,128]{1,0:T(8,128)S(1)} %fusion.62, f32[8,128,2048]{1,2,0:T(8,128)} %get-tuple-element.172, f32[8,128]{1,0:T(8,128)S(1)} %get-tuple-element.167, ...), kind=kOutput, calls=%fused_computation.67 | convolution fusion | flops 1084489728 | bytes 9969664 | tf_op jit(solution)/shard_map/while/body/eval_jaxpr/htk,thd->kd/dot_general | solution.py:50
  316.6 3.2 fusion.64
  320.2 1.8 fusion.65
  322.0 7.4 %fusion.41 = bf16[2048,1024]{0,1:T(8,128)(2,1)} fusion(bf16[2048,1024]{0,1:T(8,128)(2,1)} %fusion.39, bf16[128,8,128]{0,2,1:T(8,128)(2,1)S(1)} %bitcast.282, bf16[128,8,128]{0,2,1:T(8,128)(2,1)S(1)} %bitcast.272, f32[8,128]{1,0:T(8,128)S(1)} %fusion.63, f32[8,128,2048]{1,2,0:T(8,128)} %get-tuple-element.174, f32[8,128]{1,0:T(8,128)S(1)} %get-tuple-element.173, ...), kind=kOutput, calls=%fused_computation.69 | convolution fusion | flops 1084489728 | bytes 9969664 | tf_op jit(solution)/shard_map/while/body/eval_jaxpr/htk,thd->kd/dot_general | solution.py:50
  329.5 7.4 %fusion.43 = bf16[2048,1024]{0,1:T(8,128)(2,1)} fusion(bf16[2048,1024]{0,1:T(8,128)(2,1)} %fusion.41, bf16[128,8,128]{0,2,1:T(8,128)(2,1)S(1)} %bitcast.280, bf16[128,8,128]{0,2,1:T(8,128)(2,1)S(1)} %bitcast.269, f32[8,128]{1,0:T(8,128)S(1)} %fusion.64, f32[8,128,2048]{1,2,0:T(8,128)} %get-tuple-element.180, f32[8,128]{1,0:T(8,128)S(1)} %get-tuple-element.175, ...), kind=kOutput, calls=%fused_computation.71 | convolution fusion | flops 1084489728 | bytes 9969664 | tf_op jit(solution)/shard_map/while/body/eval_jaxpr/htk,thd->kd/dot_general | solution.py:50
  336.9 7.6 %fusion.45 = bf16[2048,1024]{0,1:T(8,128)(2,1)} fusion(bf16[2048,1024]{0,1:T(8,128)(2,1)} %fusion.43, bf16[128,8,128]{0,2,1:T(8,128)(2,1)S(1)} %bitcast.278, bf16[128,8,128]{0,2,1:T(8,128)(2,1)S(1)} %bitcast.266, f32[8,128]{1,0:T(8,128)S(1)} %fusion.65, f32[8,128,2048]{1,2,0:T(8,128)} %get-tuple-element.182, f32[8,128]{1,0:T(8,128)S(1)} %get-tuple-element.181, ...), kind=kOutput, calls=%fused_computation.73 | convolution fusion | flops 1084489728 | bytes 9969664 | tf_op jit(solution)/shard_map/while/body/eval_jaxpr/htk,thd->kd/dot_general | solution.py:50
  344.5 4.7 %fusion.47 = bf16[2048,1024]{0,1:T(8,128)(2,1)} fusion(bf16[2048,1024]{0,1:T(8,128)(2,1)} %fusion.45, bf16[8,128,2048]{1,2,0:T(8,128)(2,1)} %fusion.32, bf16[128,8,128]{0,2,1:T(8,128)(2,1)S(1)} %bitcast.276), kind=kOutput, calls=%fused_computation.75 | convolution fusion | flops 537133056 | bytes 4980736 | tf_op jit(solution)/shard_map/while/body/eval_jaxpr/htk,thd->kd/dot_general | solution.py:53
  349.2 2.3 fusion.49
  351.5 2.3 fusion.51
  353.8 2.3 fusion.53
  356.0 6.4 %copy.147 = bf16[2048,1024]{1,0:T(8,128)(2,1)} copy(bf16[2048,1024]{0,1:T(8,128)(2,1)} %fusion.53) | data formatting | bytes 8388608
  362.4 66.6 %reduce-scatter.4.cloned.1.call-done = bf16[128,1024]{1,0:T(8,128)(2,1)} async-done(((bf16[2048,1024]{1,0:T(8,128)(2,1)}), bf16[128,1024]{1,0:T(8,128)(2,1)}) %reduce-scatter.4.cloned.1.call-update) | async-done | bytes 262160
  429.0 3.9 fusion.82
  432.9 1.6 fusion.61
  434.5 1.6 fusion.66
  (53 shorter events, 6.6 us)
Async XLA Ops:
  6.5 202.4 %copy-start = (bf16[1,128,4096]{2,1,0:T(8,128)(2,1)S(1)}, bf16[1,128,4096]{2,1,0:T(8,128)(2,1)}, u32[]{:S(2)}) copy-start(bf16[1,128,4096]{2,1,0:T(8,128)(2,1)} %param.8) | copy-start | bytes 3145732
  6.5 202.4 %copy-start.13 = (f32[4096]{0:T(1024)S(1)}, f32[4096]{0:T(1024)}, u32[]{:S(2)}) copy-start(f32[4096]{0:T(1024)} %param.9) | copy-start | bytes 49156
  6.5 103.4 %all-gather.6.cloned.1.call-start = ((), (), s32[]{:S(2)}) async-start(), calls=%async_computation.2 | async-start | bytes 4456448 | tf_op jit(solution)/shard_map/all_gather | solution.py:78
  7.3 201.6 %all-gather.4.cloned.1.call-start = ((), (), s32[]{:S(2)}) async-start(), calls=%async_computation.1 | async-start | bytes 4456448 | tf_op jit(solution)/shard_map/all_gather | solution.py:77
  8.0 245.0 %all-gather.8.cloned.1.call-start = ((), (), s32[]{:S(2)}) async-start(), calls=%async_computation.3 | async-start | bytes 4456448 | tf_op jit(solution)/shard_map/all_gather | solution.py:83
  113.2 99.5 %copy-start.14 = (s32[1,32]{1,0:T(1,128)S(1)}, s32[1,32]{1,0:T(1,128)}, u32[]{:S(2)}) copy-start(s32[1,32]{1,0:T(1,128)} %param.15) | copy-start | bytes 388
  113.2 99.6 %copy-start.15 = (s32[1,16]{1,0:T(1,128)S(1)}, s32[1,16]{1,0:T(1,128)}, u32[]{:S(2)}) copy-start(s32[1,16]{1,0:T(1,128)} %param.14) | copy-start | bytes 196
  113.2 99.8 %copy-start.8 = (bf16[1,128,4096]{2,1,0:T(8,128)(2,1)S(1)}, bf16[1,128,4096]{2,1,0:T(8,128)(2,1)}, u32[]{:S(2)}) copy-start(bf16[1,128,4096]{2,1,0:T(8,128)(2,1)} %param.12) | copy-start | bytes 3145732
  212.6 216.4 %reduce-scatter.4.cloned.1.call-start = ((), (), s32[]{:S(2)}) async-start(), calls=%async_computation.4 | async-start | bytes 4456448
  259.9 6.0 %copy-start.12 = (bf16[128,1024]{0,1:T(8,128)(2,1)S(1)}, bf16[128,1024]{0,1:T(8,128)(2,1)}, u32[]{:S(2)}) copy-start(bf16[128,1024]{0,1:T(8,128)(2,1)} %get-tuple-element.164) | copy-start | bytes 786436
  272.8 6.0 %copy-start.10 = (bf16[128,1024]{0,1:T(8,128)(2,1)S(1)}, bf16[128,1024]{0,1:T(8,128)(2,1)}, u32[]{:S(2)}) copy-start(bf16[128,1024]{0,1:T(8,128)(2,1)} %get-tuple-element.157) | copy-start | bytes 786436
  298.7 6.3 %copy-start.2 = (bf16[8,128,2048]{1,2,0:T(8,128)(2,1)S(1)}, bf16[8,128,2048]{1,2,0:T(8,128)(2,1)}, u32[]{:S(2)}) copy-start(bf16[8,128,2048]{1,2,0:T(8,128)(2,1)} %fusion.33) | copy-start | bytes 12582916
  305.0 2.4 copy-start.5
  316.6 3.6 copy-start.6
  319.8 2.2 copy-start.11
  344.5 4.7 %copy-start.3 = (bf16[8,128,2048]{1,2,0:T(8,128)(2,1)S(1)}, bf16[8,128,2048]{1,2,0:T(8,128)(2,1)}, u32[]{:S(2)}) copy-start(bf16[8,128,2048]{1,2,0:T(8,128)(2,1)} %fusion.33) | copy-start | bytes 12582916
  349.2 2.3 copy-start.4
  351.5 2.3 copy-start.7
  429.0 3.9 copy-start.1
  429.0 3.9 copy-start.9
Sparse Core Ops, SparseCore 0:
  9.9 99.9 all-gather.5
  112.5 96.3 all-gather.3
  212.7 40.2 all-gather.7
  362.6 66.4 reduce-scatter.3
where the time goes:
time: 445 us; the launch traced here: 443 us
  waiting for transfers between devices  299 us (67%)
  matrix products  89.5 us (20%)
  other arithmetic  30 us (7%)
  between operations  13.3 us (3%)
  local copies, waits for them, and re-layouts  10.6 us (2%)
    all_gather x1, waiting for transfers between devices, body(): lax.all_gather(w_value, 'dp', axis=0, tiled=True)  100 us
    all_gather x1, waiting for transfers between devices, body(): lax.all_gather(w_key, 'dp', axis=0, tiled=True)  95.6 us
    unnamed x5, waiting for transfers between devices  68 us
    all_gather x1, waiting for transfers between devices, body(): all_kv = lax.all_gather(local_kv, 'ctx', axis=0, tiled=True)  35.1 us
    dot_general x4, matrix products, grad_block(): jnp.einsum('htk,thd->kd', score_grad, query_group, preferred_element_type...  29.8 us
    sub x4, matrix products, attend(): raised = jnp.exp(scores - row_max[None, :, :, None])  27.6 us
    convert_element_type x4, other arithmetic, attend(): probs_half = soft_probs.astype(jnp.bfloat16)  24.4 us
    dot_general x4, matrix products, grad_block(): jnp.einsum('htk,thd->kd', prob_half, dout_group, preferred_element_type=j...  11.5 us
  transfers between devices with their start and end apart: 4, of which 4 were waited for; matrix products, arithmetic and copies ran while one was open for 2% of the time, Pallas kernels for 0%

commit v1 on v0

--- a/solution.py
+++ b/solution.py
@@ -61,6 +61,16 @@
     return (key_grad.reshape(seq_len, head_size), value_grad.reshape(seq_len, head_size))
 
 
+def gather_weights(local_w, ctx_ways):
+    shard_rows = local_w.shape[0]
+    piece_rows = shard_rows // ctx_ways
+    start = lax.axis_index("ctx") * piece_rows
+    piece = lax.dynamic_slice_in_dim(local_w, start, piece_rows, axis=0)
+    by_shard = lax.all_gather(piece, "dp", axis=0, tiled=False)
+    full = lax.all_gather(by_shard, "ctx", axis=1, tiled=False)
+    return full.reshape(-1, local_w.shape[1])
+
+
 def body(embeds, norm_gain, w_key, w_value, queries, d_out, block_doc, slot_order):
     embed_rows = embeds[0]
     tok_rows = embed_rows.shape[0]
@@ -73,14 +83,12 @@
     as_float = embed_rows.astype(jnp.float32)
     inv_rms = lax.rsqrt(jnp.mean(as_float * as_float, axis=-1, keepdims=True) + 1e-05)
     normed = (as_float * inv_rms * norm_gain).astype(jnp.bfloat16)
-    pieces = (
-        lax.all_gather(w_key, "dp", axis=0, tiled=True),
-        lax.all_gather(w_value, "dp", axis=0, tiled=True),
-    )
+    pieces = gather_weights(jnp.concatenate([w_key, w_value], axis=1), ctx_ways)
+    pieces = (pieces[:, :kv_width], pieces[:, kv_width:])
     key_proj = jnp.dot(normed, pieces[0], preferred_element_type=jnp.float32)
     value_proj = jnp.dot(normed, pieces[1], preferred_element_type=jnp.float32)
-    local_kv = jnp.concatenate([key_proj, value_proj], axis=1).astype(jnp.bfloat16)
-    all_kv = lax.all_gather(local_kv, "ctx", axis=0, tiled=True)
+    key_proj = key_proj.astype(jnp.bfloat16)
+    value_proj = value_proj.astype(jnp.bfloat16)
     row_ids = jnp.arange(seq_len, dtype=jnp.int32)
     slot_hit = (row_ids // half_len)[:, None] == jnp.arange(2 * ctx_ways, dtype=jnp.int32)[None, :]
     key_pos = (
@@ -102,21 +110,23 @@
         last_col = (kv_head + 1) * group_size * HEAD
         query_group = queries[0][:, first_col:last_col].reshape(tok_rows, group_size, HEAD)
         dout_group = d_out[0][:, first_col:last_col].reshape(tok_rows, group_size, HEAD)
-        key_group = all_kv[:, kv_head * HEAD : (kv_head + 1) * HEAD]
-        value_group = all_kv[:, kv_width + kv_head * HEAD : kv_width + (kv_head + 1) * HEAD]
+        head_kv = jnp.concatenate(
+            [key_proj[:, kv_head * HEAD : (kv_head + 1) * HEAD],
+             value_proj[:, kv_head * HEAD : (kv_head + 1) * HEAD]], axis=1)
+        head_kv = lax.all_gather(head_kv, "ctx", axis=0, tiled=True)
+        key_group = head_kv[:, :HEAD]
+        value_group = head_kv[:, HEAD:]
         key_grad, value_grad = attend(
             query_group, dout_group, key_group, value_group, allowed, seq_len, score_scale
         )
-        key_grads.append(key_grad)
-        value_grads.append(value_grad)
-    grad_terms = jnp.concatenate(key_grads + value_grads, axis=1)
-    own_sum = lax.psum_scatter(
-        grad_terms.astype(jnp.bfloat16), "ctx", scatter_dimension=0, tiled=True
-    )
-    key_half = own_sum[:, :kv_width]
-    value_half = own_sum[:, kv_width:]
+        head_sum = lax.psum_scatter(
+            jnp.concatenate([key_grad, value_grad], axis=1).astype(jnp.bfloat16),
+            "ctx", scatter_dimension=0, tiled=True)
+        key_grads.append(head_sum[:, :HEAD])
+        value_grads.append(head_sum[:, HEAD:])
+    key_half = jnp.concatenate(key_grads, axis=1)
+    value_half = jnp.concatenate(value_grads, axis=1)
     contract = (((1,), (1,)), ((), ()))
-    pieces = lax.all_gather((w_key, w_value), "dp", axis=0, tiled=True)
     grad_normed = lax.dot_general(
         key_half, pieces[0], contract, preferred_element_type=jnp.float32
     ) + lax.dot_general(value_half, pieces[1], contract, preferred_element_type=jnp.float32)

time: 445 us -> 548 us (1.23); the launches traced: 443 us -> 538 us
  waiting for transfers between devices: 299 us -> 364 us
  blocking collectives: 0 us -> 42.7 us
  matrix products: 89.5 us -> 76.9 us
    unnamed x5 -> x13, waiting for transfers between devices: 68 us -> 238 us
    all_gather x3 -> x5, waiting for transfers between devices: 231 us -> 127 us  [the longest x4 71.8 us: body(): head_kv = lax.all_gather(head_kv, 'ctx', axis=0, tiled=True)]
    all_gather x0 -> x1, blocking collectives: none -> 42.7 us  [gather_weights(): by_shard = lax.all_gather(piece, 'dp', axis=0, tiled=False)]
    convert_element_type x4, other arithmetic: 24.4 us -> 16.7 us  [attend(): probs_half = soft_probs.astype(jnp.bfloat16)]
    unnamed x4, matrix products: 8.88 us -> 3.14 us
    dot_general x4, matrix products: 11.5 us -> 5.95 us  [grad_block(): jnp.einsum('htk,thd->kd', prob_half, dout_group, preferred_element_type=j...]
  transfers between devices with their start and end apart: 4 -> 9, of which waited for: 4 -> 9; matrix products, arithmetic and copies ran while one was open for 2% -> 18% of each run, Pallas kernels for 0% -> 0%
where the time goes in v1:
time: 548 us; the launch traced here: 538 us
  waiting for transfers between devices  364 us (66%)
  matrix products  76.9 us (14%)
  blocking collectives  42.7 us (8%)
  other arithmetic  25.1 us (5%)
  between operations  14.1 us (3%)
  local copies, waits for them, and re-layouts  13.8 us (3%)
    unnamed x13, waiting for transfers between devices  238 us
    all_gather x4, waiting for transfers between devices, body(): head_kv = lax.all_gather(head_kv, 'ctx', axis=0, tiled=True)  71.8 us
    all_gather x1, waiting for transfers between devices, gather_weights(): full = lax.all_gather(by_shard, 'ctx', axis=1, tiled=False)  55 us
    all_gather x1, blocking collectives, gather_weights(): by_shard = lax.all_gather(piece, 'dp', axis=0, tiled=False)  42.7 us
    sub x4, matrix products, attend(): raised = jnp.exp(scores - row_max[None, :, :, None])  27.6 us
    dot_general x4, matrix products, grad_block(): jnp.einsum('htk,thd->kd', score_grad, query_group, preferred_element_type...  26.5 us
    convert_element_type x4, other arithmetic, attend(): probs_half = soft_probs.astype(jnp.bfloat16)  16.7 us
  transfers between devices with their start and end apart: 9, of which 9 were waited for; matrix products, arithmetic and copies ran while one was open for 18% of the time, Pallas kernels for 0%

profile of v1, /device:TPU:1, one launch (start us, length us, event | category | flops | bytes accessed | tf_op | source)
XLA Modules:
  0.0 537.8 jit_solution(9684082943269075039)
XLA Ops:
  7.4 42.7 %all-gather = bf16[256,1024]{1,0:T(8,128)(2,1)} all-gather(bf16[16,1024]{1,0:T(8,128)(2,1)S(1)} %fusion.100), channel_id=2, replica_groups=mesh['dp'=16,'ctx'=16] {'dp'}, dimensions={0}, use_global_device_ids=true | all-gather | bytes 557056 | tf_op jit(solution)/shard_map/all_gather | solution.py:69
  50.1 1.5 fusion.58
  51.7 55.0 %all-gather.16.cloned.1.call-done = bf16[16,256,1024]{2,1,0:T(8,128)(2,1)} async-done(((bf16[16,16,1024]{2,1,0:T(8,128)(2,1)}), bf16[16,256,1024]{2,1,0:T(8,128)(2,1)}) %all-gather.16.cloned.1.call-update) | async-done | bytes 8388624 | tf_op jit(solution)/shard_map/all_gather | solution.py:70
  106.7 3.3 fusion.65
  110.0 2.9 fusion.68
  116.2 1.6 copy.87
  121.8 27.7 %all-gather.8.cloned.1.call-done = bf16[2048,256]{1,0:T(8,128)(2,1)} async-done(((bf16[128,256]{1,0:T(8,128)(2,1)}), bf16[2048,256]{1,0:T(8,128)(2,1)}) %all-gather.8.cloned.1.call-update) | async-done | bytes 1048592 | tf_op jit(solution)/shard_map/all_gather | solution.py:116
  149.5 6.9 %fusion.133 = (f32[8,128]{1,0:T(8,128)S(1)}, f32[8,128,2048]{1,2,0:T(8,128)}) fusion(pred[128,2048]{0,1:T(8,128)(4,1)S(1)} %compare_and_fusion, bf16[128,8,128]{0,2,1:T(8,128)(2,1)} %bitcast.270, bf16[2048,256]{1,0:T(8,128)(2,1)} %all-gather.8.cloned.1.call-done), kind=kOutput, calls=%fused_computation.189 | convolution fusion | flops 545261568 | bytes 9441280 | tf_op jit(solution)/shard_map/sub | solution.py:31
  156.4 4.2 fusion.39
  160.5 1.5 fusion.46
  162.9 6.7 %fusion.45 = bf16[2048,128]{0,1:T(8,128)(2,1)S(1)} fusion(bf16[128,8,128]{0,2,1:T(8,128)(2,1)S(1)} %bitcast.271, bf16[128,8,128]{0,2,1:T(8,128)(2,1)} %bitcast.274, f32[8,128]{1,0:T(8,128)S(1)} %fusion.61, f32[8,128,2048]{1,2,0:T(8,128)} %get-tuple-element.201, f32[8,128]{1,0:T(8,128)S(1)} %get-tuple-element.200, ...), kind=kOutput, calls=%fused_computation.73 | convolution fusion | flops 1084489728 | bytes 9969664 | tf_op jit(solution)/shard_map/while/body/eval_jaxpr/htk,thd->kd/dot_general | solution.py:50
  171.2 14.8 %all-gather.10.cloned.1.call-done = bf16[2048,256]{1,0:T(8,128)(2,1)} async-done(((bf16[128,256]{1,0:T(8,128)(2,1)}), bf16[2048,256]{1,0:T(8,128)(2,1)}) %all-gather.10.cloned.1.call-update) | async-done | bytes 1048592 | tf_op jit(solution)/shard_map/all_gather | solution.py:116
  186.0 6.9 %fusion.134 = (f32[8,128]{1,0:T(8,128)S(1)}, f32[8,128,2048]{1,2,0:T(8,128)}) fusion(pred[128,2048]{0,1:T(8,128)(4,1)S(1)} %compare_and_fusion, bf16[128,8,128]{0,2,1:T(8,128)(2,1)} %bitcast.265, bf16[2048,256]{1,0:T(8,128)(2,1)} %all-gather.10.cloned.1.call-done), kind=kOutput, calls=%fused_computation.190 | convolution fusion | flops 545261568 | bytes 9441280 | tf_op jit(solution)/shard_map/sub | solution.py:31
  192.9 4.2 fusion.40
  197.1 1.5 fusion.48
  199.4 6.6 %fusion.47 = bf16[2048,128]{0,1:T(8,128)(2,1)S(1)} fusion(bf16[128,8,128]{0,2,1:T(8,128)(2,1)S(1)} %bitcast.266, bf16[128,8,128]{0,2,1:T(8,128)(2,1)S(1)} %bitcast.269, f32[8,128]{1,0:T(8,128)S(1)} %fusion.62, f32[8,128,2048]{1,2,0:T(8,128)} %get-tuple-element.203, f32[8,128]{1,0:T(8,128)S(1)} %get-tuple-element.202, ...), kind=kOutput, calls=%fused_computation.75 | convolution fusion | flops 1084489728 | bytes 9969664 | tf_op jit(solution)/shard_map/while/body/eval_jaxpr/htk,thd->kd/dot_general | solution.py:50
  207.8 14.7 %all-gather.12.cloned.1.call-done = bf16[2048,256]{1,0:T(8,128)(2,1)} async-done(((bf16[128,256]{1,0:T(8,128)(2,1)}), bf16[2048,256]{1,0:T(8,128)(2,1)}) %all-gather.12.cloned.1.call-update) | async-done | bytes 1048592 | tf_op jit(solution)/shard_map/all_gather | solution.py:116
  222.5 6.9 %fusion.135 = (f32[8,128]{1,0:T(8,128)S(1)}, f32[8,128,2048]{1,2,0:T(8,128)}) fusion(pred[128,2048]{0,1:T(8,128)(4,1)S(1)} %compare_and_fusion, bf16[128,8,128]{0,2,1:T(8,128)(2,1)} %bitcast.260, bf16[2048,256]{1,0:T(8,128)(2,1)} %all-gather.12.cloned.1.call-done), kind=kOutput, calls=%fused_computation.191 | convolution fusion | flops 545261568 | bytes 9441280 | tf_op jit(solution)/shard_map/sub | solution.py:31
  229.4 4.2 fusion.41
  233.6 1.5 fusion.50
  235.9 6.6 %fusion.49 = bf16[2048,128]{0,1:T(8,128)(2,1)S(1)} fusion(bf16[128,8,128]{0,2,1:T(8,128)(2,1)S(1)} %bitcast.261, bf16[128,8,128]{0,2,1:T(8,128)(2,1)S(1)} %bitcast.264, f32[8,128]{1,0:T(8,128)S(1)} %fusion.63, f32[8,128,2048]{1,2,0:T(8,128)} %get-tuple-element.205, f32[8,128]{1,0:T(8,128)S(1)} %get-tuple-element.204, ...), kind=kOutput, calls=%fused_computation.77 | convolution fusion | flops 1084489728 | bytes 9969664 | tf_op jit(solution)/shard_map/while/body/eval_jaxpr/htk,thd->kd/dot_general | solution.py:50
  244.3 14.7 %all-gather.14.cloned.1.call-done = bf16[2048,256]{1,0:T(8,128)(2,1)} async-done(((bf16[128,256]{1,0:T(8,128)(2,1)}), bf16[2048,256]{1,0:T(8,128)(2,1)}) %all-gather.14.cloned.1.call-update) | async-done | bytes 1048592 | tf_op jit(solution)/shard_map/all_gather | solution.py:116
  258.9 6.9 %fusion.136 = (f32[8,128]{1,0:T(8,128)S(1)}, f32[8,128,2048]{1,2,0:T(8,128)}) fusion(pred[128,2048]{0,1:T(8,128)(4,1)S(1)} %compare_and_fusion, bf16[128,8,128]{0,2,1:T(8,128)(2,1)} %bitcast.255, bf16[2048,256]{1,0:T(8,128)(2,1)} %all-gather.14.cloned.1.call-done), kind=kOutput, calls=%fused_computation.192 | convolution fusion | flops 545261568 | bytes 9441280 | tf_op jit(solution)/shard_map/sub | solution.py:31
  265.8 4.2 fusion.42
  272.3 6.6 %fusion.51 = bf16[2048,128]{0,1:T(8,128)(2,1)S(1)} fusion(bf16[128,8,128]{0,2,1:T(8,128)(2,1)S(1)} %bitcast.256, bf16[128,8,128]{0,2,1:T(8,128)(2,1)S(1)} %bitcast.259, f32[8,128]{1,0:T(8,128)S(1)} %fusion.64, f32[8,128,2048]{1,2,0:T(8,128)} %get-tuple-element.216, f32[8,128]{1,0:T(8,128)S(1)} %get-tuple-element.206, ...), kind=kOutput, calls=%fused_computation.79 | convolution fusion | flops 1084489728 | bytes 9969664 | tf_op jit(solution)/shard_map/while/body/eval_jaxpr/htk,thd->kd/dot_general | solution.py:50
  280.3 42.1 %reduce-scatter.13.cloned.1.call-done = bf16[128,256]{1,0:T(8,128)(2,1)} async-done(((bf16[2048,256]{1,0:T(8,128)(2,1)}), bf16[128,256]{1,0:T(8,128)(2,1)}) %reduce-scatter.13.cloned.1.call-update) | async-done | bytes 65552
  323.4 65.0 %reduce-scatter.15.cloned.1.call-done = bf16[128,256]{1,0:T(8,128)(2,1)} async-done(((bf16[2048,256]{1,0:T(8,128)(2,1)}), bf16[128,256]{1,0:T(8,128)(2,1)}) %reduce-scatter.15.cloned.1.call-update) | async-done | bytes 65552
  389.3 65.1 %reduce-scatter.17.cloned.1.call-done = bf16[128,256]{1,0:T(8,128)(2,1)} async-done(((bf16[2048,256]{1,0:T(8,128)(2,1)}), bf16[128,256]{1,0:T(8,128)(2,1)}) %reduce-scatter.17.cloned.1.call-update) | async-done | bytes 65552
  455.3 65.1 %reduce-scatter.19.cloned.1.call-done = bf16[128,256]{1,0:T(8,128)(2,1)} async-done(((bf16[2048,256]{1,0:T(8,128)(2,1)}), bf16[128,256]{1,0:T(8,128)(2,1)}) %reduce-scatter.19.cloned.1.call-update) | async-done | bytes 65552
  521.8 3.7 fusion.35
  525.5 3.8 fusion.60
  529.3 1.6 fusion.71
  (95 shorter events, 23.2 us)
Async XLA Ops:
  6.5 103.4 %copy-start = (bf16[1,128,4096]{2,1,0:T(8,128)(2,1)S(1)}, bf16[1,128,4096]{2,1,0:T(8,128)(2,1)}, u32[]{:S(2)}) copy-start(bf16[1,128,4096]{2,1,0:T(8,128)(2,1)} %param.8) | copy-start | bytes 3145732
  6.5 103.5 %copy-start.10 = (f32[4096]{0:T(1024)S(1)}, f32[4096]{0:T(1024)}, u32[]{:S(2)}) copy-start(f32[4096]{0:T(1024)} %param.9) | copy-start | bytes 49156
  6.5 100.1 %all-gather.16.cloned.1.call-start = ((), (), s32[]{:S(2)}) async-start(), calls=%async_computation.8 | async-start | bytes 8912896 | tf_op jit(solution)/shard_map/all_gather | solution.py:70
  50.1 99.4 %all-gather.8.cloned.1.call-start = ((), (), s32[]{:S(2)}) async-start(), calls=%async_computation.4 | async-start | bytes 1114112 | tf_op jit(solution)/shard_map/all_gather | solution.py:116
  51.6 63.5 %copy-start.11 = (s32[1,32]{1,0:T(1,128)S(1)}, s32[1,32]{1,0:T(1,128)}, u32[]{:S(2)}) copy-start(s32[1,32]{1,0:T(1,128)} %param.15) | copy-start | bytes 388
  51.7 63.7 %copy-start.12 = (s32[1,16]{1,0:T(1,128)S(1)}, s32[1,16]{1,0:T(1,128)}, u32[]{:S(2)}) copy-start(s32[1,16]{1,0:T(1,128)} %param.14) | copy-start | bytes 196
  51.7 63.9 %copy-start.1 = (bf16[1,128,4096]{2,1,0:T(8,128)(2,1)S(1)}, bf16[1,128,4096]{2,1,0:T(8,128)(2,1)}, u32[]{:S(2)}) copy-start(bf16[1,128,4096]{2,1,0:T(8,128)(2,1)} %param.12) | copy-start | bytes 3145732
  113.7 72.3 %all-gather.10.cloned.1.call-start = ((), (), s32[]{:S(2)}) async-start(), calls=%async_computation.5 | async-start | bytes 1114112 | tf_op jit(solution)/shard_map/all_gather | solution.py:116
  114.4 108.1 %all-gather.12.cloned.1.call-start = ((), (), s32[]{:S(2)}) async-start(), calls=%async_computation.6 | async-start | bytes 1114112 | tf_op jit(solution)/shard_map/all_gather | solution.py:116
  115.1 143.8 %all-gather.14.cloned.1.call-start = ((), (), s32[]{:S(2)}) async-start(), calls=%async_computation.7 | async-start | bytes 1114112 | tf_op jit(solution)/shard_map/all_gather | solution.py:116
  119.8 42.3 %copy-start.9 = (bf16[128,1024]{0,1:T(8,128)(2,1)}, bf16[128,1024]{0,1:T(8,128)(2,1)S(1)}, u32[]{:S(2)}) copy-start(bf16[128,1024]{0,1:T(8,128)(2,1)S(1)} %get-tuple-element.147) | copy-start | bytes 786436
  121.7 200.7 %reduce-scatter.13.cloned.1.call-start = ((), (), s32[]{:S(2)}) async-start(), calls=%async_computation.9 | async-start | bytes 1114112
  156.3 5.7 %copy-start.16 = (bf16[2048,256]{1,0:T(8,128)(2,1)S(1)}, bf16[2048,256]{1,0:T(8,128)(2,1)}, u32[]{:S(2)}) copy-start(bf16[2048,256]{1,0:T(8,128)(2,1)} %all-gather.8.cloned.1.call-done) | copy-start | bytes 3145732
  160.5 2.3 copy-start.8
  171.0 217.4 %reduce-scatter.15.cloned.1.call-start = ((), (), s32[]{:S(2)}) async-start(), calls=%async_computation.10 | async-start | bytes 1114112
  192.9 4.2 copy-start.7
  192.9 5.7 %copy-start.15 = (bf16[2048,256]{1,0:T(8,128)(2,1)S(1)}, bf16[2048,256]{1,0:T(8,128)(2,1)}, u32[]{:S(2)}) copy-start(bf16[2048,256]{1,0:T(8,128)(2,1)} %all-gather.10.cloned.1.call-done) | copy-start | bytes 3145732
  197.1 2.3 copy-start.6
  207.5 246.9 %reduce-scatter.17.cloned.1.call-start = ((), (), s32[]{:S(2)}) async-start(), calls=%async_computation.11 | async-start | bytes 1114112
  229.4 4.2 copy-start.5
  229.4 5.7 %copy-start.13 = (bf16[2048,256]{1,0:T(8,128)(2,1)S(1)}, bf16[2048,256]{1,0:T(8,128)(2,1)}, u32[]{:S(2)}) copy-start(bf16[2048,256]{1,0:T(8,128)(2,1)} %all-gather.12.cloned.1.call-done) | copy-start | bytes 3145732
  233.5 2.3 copy-start.4
  244.0 276.4 %reduce-scatter.19.cloned.1.call-start = ((), (), s32[]{:S(2)}) async-start(), calls=%async_computation.12 | async-start | bytes 1114112
  265.8 4.2 copy-start.3
  265.8 5.7 %copy-start.14 = (bf16[2048,256]{1,0:T(8,128)(2,1)S(1)}, bf16[2048,256]{1,0:T(8,128)(2,1)}, u32[]{:S(2)}) copy-start(bf16[2048,256]{1,0:T(8,128)(2,1)} %all-gather.14.cloned.1.call-done) | copy-start | bytes 3145732
  270.0 2.3 copy-start.2
Sparse Core Ops, SparseCore 0:
  50.2 56.4 all-gather.15
  113.8 35.6 all-gather.7
  151.3 34.6 all-gather.9
  187.7 34.6 all-gather.11
  224.2 34.7 all-gather.13
  261.3 61.1 reduce-scatter.12
  325.0 63.3 reduce-scatter.14
  390.9 63.4 reduce-scatter.16
  456.9 63.4 reduce-scatter.18

commit v2 on v0

--- a/solution.py
+++ b/solution.py
@@ -61,6 +61,16 @@
     return (key_grad.reshape(seq_len, head_size), value_grad.reshape(seq_len, head_size))
 
 
+def gather_weights(local_w, ctx_ways):
+    shard_rows = local_w.shape[0]
+    piece_rows = shard_rows // ctx_ways
+    start = lax.axis_index("ctx") * piece_rows
+    piece = lax.dynamic_slice_in_dim(local_w, start, piece_rows, axis=0)
+    by_shard = lax.all_gather(piece, "dp", axis=0, tiled=False)
+    full = lax.all_gather(by_shard, "ctx", axis=1, tiled=False)
+    return full.reshape(-1, local_w.shape[1])
+
+
 def body(embeds, norm_gain, w_key, w_value, queries, d_out, block_doc, slot_order):
     embed_rows = embeds[0]
     tok_rows = embed_rows.shape[0]
@@ -73,10 +83,8 @@
     as_float = embed_rows.astype(jnp.float32)
     inv_rms = lax.rsqrt(jnp.mean(as_float * as_float, axis=-1, keepdims=True) + 1e-05)
     normed = (as_float * inv_rms * norm_gain).astype(jnp.bfloat16)
-    pieces = (
-        lax.all_gather(w_key, "dp", axis=0, tiled=True),
-        lax.all_gather(w_value, "dp", axis=0, tiled=True),
-    )
+    pieces = gather_weights(jnp.concatenate([w_key, w_value], axis=1), ctx_ways)
+    pieces = (pieces[:, :kv_width], pieces[:, kv_width:])
     key_proj = jnp.dot(normed, pieces[0], preferred_element_type=jnp.float32)
     value_proj = jnp.dot(normed, pieces[1], preferred_element_type=jnp.float32)
     local_kv = jnp.concatenate([key_proj, value_proj], axis=1).astype(jnp.bfloat16)
@@ -116,7 +124,6 @@
     key_half = own_sum[:, :kv_width]
     value_half = own_sum[:, kv_width:]
     contract = (((1,), (1,)), ((), ()))
-    pieces = lax.all_gather((w_key, w_value), "dp", axis=0, tiled=True)
     grad_normed = lax.dot_general(
         key_half, pieces[0], contract, preferred_element_type=jnp.float32
     ) + lax.dot_general(value_half, pieces[1], contract, preferred_element_type=jnp.float32)

time: 445 us -> 349 us (0.78)
  waiting for transfers between devices: 299 us -> 157 us
  blocking collectives: 0 us -> 42.7 us
    all_gather x2 -> x1, waiting for transfers between devices: 196 us -> 54.9 us  [gather_weights(): full = lax.all_gather(by_shard, 'ctx', axis=1, tiled=False)]
    all_gather x0 -> x1, blocking collectives: none -> 42.7 us  [gather_weights(): by_shard = lax.all_gather(piece, 'dp', axis=0, tiled=False)]
    unnamed x5 -> x4, waiting for transfers between devices: 68 us -> 66.6 us
    unnamed x35 -> x33, local copies, waits for them, and re-layouts: 9.45 us -> 9.46 us
  transfers between devices with their start and end apart: 4 -> 3, of which waited for: 4 -> 3; matrix products, arithmetic and copies ran while one was open for 2% -> 2% of each run, Pallas kernels for 0% -> 0%
where the time goes in v2:
time: 349 us; the launch traced here: 346 us
  waiting for transfers between devices  157 us (45%)
  matrix products  91.7 us (26%)
  blocking collectives  42.7 us (12%)
  other arithmetic  30.8 us (9%)
  between operations  13.3 us (4%)
  local copies, waits for them, and re-layouts  10.6 us (3%)
    unnamed x4, waiting for transfers between devices  66.6 us
    all_gather x1, waiting for transfers between devices, gather_weights(): full = lax.all_gather(by_shard, 'ctx', axis=1, tiled=False)  54.9 us
    all_gather x1, blocking collectives, gather_weights(): by_shard = lax.all_gather(piece, 'dp', axis=0, tiled=False)  42.7 us
    all_gather x1, waiting for transfers between devices, body(): all_kv = lax.all_gather(local_kv, 'ctx', axis=0, tiled=True)  35.5 us
    dot_general x4, matrix products, grad_block(): jnp.einsum('htk,thd->kd', score_grad, query_group, preferred_element_type...  29.8 us
    sub x4, matrix products, attend(): raised = jnp.exp(scores - row_max[None, :, :, None])  27.6 us
    convert_element_type x4, other arithmetic, attend(): probs_half = soft_probs.astype(jnp.bfloat16)  24.4 us
    dot_general x4, matrix products, grad_block(): jnp.einsum('htk,thd->kd', prob_half, dout_group, preferred_element_type=j...  11.5 us
  transfers between devices with their start and end apart: 3, of which 3 were waited for; matrix products, arithmetic and copies ran while one was open for 2% of the time, Pallas kernels for 0%

profile of v2, /device:TPU:1, one launch (start us, length us, event | category | flops | bytes accessed | tf_op | source)
XLA Modules:
  0.0 346.2 jit_solution(5638549547331666412)
XLA Ops:
  7.3 42.7 %all-gather = bf16[256,1024]{1,0:T(8,128)(2,1)} all-gather(bf16[16,1024]{1,0:T(8,128)(2,1)S(1)} %fusion.96), channel_id=2, replica_groups=mesh['dp'=16,'ctx'=16] {'dp'}, dimensions={0}, use_global_device_ids=true | all-gather | bytes 557056 | tf_op jit(solution)/shard_map/all_gather | solution.py:69
  50.1 1.6 fusion.66
  51.7 54.9 %all-gather.7.cloned.1.call-done = bf16[16,256,1024]{2,1,0:T(8,128)(2,1)} async-done(((bf16[16,16,1024]{2,1,0:T(8,128)(2,1)}), bf16[16,256,1024]{2,1,0:T(8,128)(2,1)}) %all-gather.7.cloned.1.call-update) | async-done | bytes 8388624 | tf_op jit(solution)/shard_map/all_gather | solution.py:70
  106.6 3.3 fusion.73
  109.9 3.0 fusion.76
  114.9 1.6 copy.87
  119.0 35.5 %all-gather.5.cloned.1.call-done = bf16[2048,1024]{1,0:T(8,128)(2,1)} async-done(((bf16[128,1024]{1,0:T(8,128)(2,1)}), bf16[2048,1024]{1,0:T(8,128)(2,1)}) %all-gather.5.cloned.1.call-update) | async-done | bytes 4194320 | tf_op jit(solution)/shard_map/all_gather | solution.py:91
  154.4 6.9 %fusion.122 = (f32[8,128]{1,0:T(8,128)S(1)}, f32[8,128,2048]{1,2,0:T(8,128)}) fusion(pred[128,2048]{0,1:T(8,128)(4,1)S(1)} %compare_and_fusion, bf16[128,8,128]{0,2,1:T(8,128)(2,1)} %bitcast.284, bf16[2048,1024]{1,0:T(8,128)(2,1)} %all-gather.5.cloned.1.call-done), kind=kOutput, calls=%fused_computation.171 | convolution fusion | flops 545261568 | bytes 9441280 | tf_op jit(solution)/shard_map/sub | solution.py:31
  161.3 6.0 %fusion.40 = bf16[8,128,2048]{1,2,0:T(8,128)(2,1)} fusion(f32[8,128,2048]{1,2,0:T(8,128)} %get-tuple-element.174, f32[8,128]{1,0:T(8,128)S(1)} %get-tuple-element.173), kind=kLoop, calls=%fused_computation.57 | loop fusion | flops 4194304 | bytes 12587008 | tf_op jit(solution)/shard_map/convert_element_type | solution.py:33
  167.4 6.8 %fusion.121 = (f32[8,128]{1,0:T(8,128)S(1)}, f32[8,128,2048]{1,2,0:T(8,128)}) fusion(pred[128,2048]{0,1:T(8,128)(4,1)S(1)} %compare_and_fusion, bf16[128,8,128]{0,2,1:T(8,128)(2,1)S(1)} %bitcast.286, bf16[2048,1024]{1,0:T(8,128)(2,1)} %all-gather.5.cloned.1.call-done), kind=kOutput, calls=%fused_computation.170 | convolution fusion | flops 545261568 | bytes 9441280 | tf_op jit(solution)/shard_map/sub | solution.py:31
  174.2 6.0 %fusion.39 = bf16[8,128,2048]{1,2,0:T(8,128)(2,1)} fusion(f32[8,128,2048]{1,2,0:T(8,128)} %get-tuple-element.172, f32[8,128]{1,0:T(8,128)S(1)} %get-tuple-element.167), kind=kLoop, calls=%fused_computation.56 | loop fusion | flops 4194304 | bytes 12587008 | tf_op jit(solution)/shard_map/convert_element_type | solution.py:33
  180.2 6.8 %fusion.123 = (f32[8,128]{1,0:T(8,128)S(1)}, f32[8,128,2048]{1,2,0:T(8,128)}) fusion(pred[128,2048]{0,1:T(8,128)(4,1)S(1)} %compare_and_fusion, bf16[128,8,128]{0,2,1:T(8,128)(2,1)S(1)} %bitcast.282, bf16[2048,1024]{1,0:T(8,128)(2,1)} %all-gather.5.cloned.1.call-done), kind=kOutput, calls=%fused_computation.172 | convolution fusion | flops 545261568 | bytes 9441280 | tf_op jit(solution)/shard_map/sub | solution.py:31
  187.1 6.0 %fusion.41 = bf16[8,128,2048]{1,2,0:T(8,128)(2,1)} fusion(f32[8,128,2048]{1,2,0:T(8,128)} %get-tuple-element.180, f32[8,128]{1,0:T(8,128)S(1)} %get-tuple-element.175), kind=kLoop, calls=%fused_computation.58 | loop fusion | flops 4194304 | bytes 12587008 | tf_op jit(solution)/shard_map/convert_element_type | solution.py:33
  193.1 7.1 %fusion.124 = (f32[8,128]{1,0:T(8,128)S(1)}, f32[8,128,2048]{1,2,0:T(8,128)}) fusion(pred[128,2048]{0,1:T(8,128)(4,1)S(1)} %compare_and_fusion, bf16[128,8,128]{0,2,1:T(8,128)(2,1)S(1)} %bitcast.280, bf16[2048,1024]{1,0:T(8,128)(2,1)} %all-gather.5.cloned.1.call-done), kind=kOutput, calls=%fused_computation.173 | convolution fusion | flops 545261568 | bytes 9441280 | tf_op jit(solution)/shard_map/sub | solution.py:31
  200.2 6.3 %fusion.42 = bf16[8,128,2048]{1,2,0:T(8,128)(2,1)} fusion(f32[8,128,2048]{1,2,0:T(8,128)} %get-tuple-element.182, f32[8,128]{1,0:T(8,128)S(1)} %get-tuple-element.181), kind=kLoop, calls=%fused_computation.59 | loop fusion | flops 4194304 | bytes 12587008 | tf_op jit(solution)/shard_map/convert_element_type | solution.py:33
  206.4 2.0 fusion.70
  208.8 1.8 fusion.69
  210.6 7.4 %fusion.46 = bf16[2048,1024]{0,1:T(8,128)(2,1)} fusion(bf16[128,8,128]{0,2,1:T(8,128)(2,1)S(1)} %bitcast.287, bf16[128,8,128]{0,2,1:T(8,128)(2,1)S(1)} %bitcast.278, f32[8,128]{1,0:T(8,128)S(1)} %fusion.69, f32[8,128,2048]{1,2,0:T(8,128)} %get-tuple-element.172, f32[8,128]{1,0:T(8,128)S(1)} %get-tuple-element.167, ...), kind=kOutput, calls=%fused_computation.74 | convolution fusion | flops 1084489728 | bytes 9969664 | tf_op jit(solution)/shard_map/while/body/eval_jaxpr/htk,thd->kd/dot_general | solution.py:50
  218.0 3.2 fusion.71
  221.6 1.8 fusion.72
  223.5 7.4 %fusion.48 = bf16[2048,1024]{0,1:T(8,128)(2,1)} fusion(bf16[2048,1024]{0,1:T(8,128)(2,1)} %fusion.46, bf16[128,8,128]{0,2,1:T(8,128)(2,1)S(1)} %bitcast.285, bf16[128,8,128]{0,2,1:T(8,128)(2,1)S(1)} %bitcast.275, f32[8,128]{1,0:T(8,128)S(1)} %fusion.70, f32[8,128,2048]{1,2,0:T(8,128)} %get-tuple-element.174, f32[8,128]{1,0:T(8,128)S(1)} %get-tuple-element.173, ...), kind=kOutput, calls=%fused_computation.76 | convolution fusion | flops 1084489728 | bytes 9969664 | tf_op jit(solution)/shard_map/while/body/eval_jaxpr/htk,thd->kd/dot_general | solution.py:50
  230.9 7.4 %fusion.50 = bf16[2048,1024]{0,1:T(8,128)(2,1)} fusion(bf16[2048,1024]{0,1:T(8,128)(2,1)} %fusion.48, bf16[128,8,128]{0,2,1:T(8,128)(2,1)S(1)} %bitcast.283, bf16[128,8,128]{0,2,1:T(8,128)(2,1)S(1)} %bitcast.272, f32[8,128]{1,0:T(8,128)S(1)} %fusion.71, f32[8,128,2048]{1,2,0:T(8,128)} %get-tuple-element.180, f32[8,128]{1,0:T(8,128)S(1)} %get-tuple-element.175, ...), kind=kOutput, calls=%fused_computation.78 | convolution fusion | flops 1084489728 | bytes 9969664 | tf_op jit(solution)/shard_map/while/body/eval_jaxpr/htk,thd->kd/dot_general | solution.py:50
  238.3 7.6 %fusion.52 = bf16[2048,1024]{0,1:T(8,128)(2,1)} fusion(bf16[2048,1024]{0,1:T(8,128)(2,1)} %fusion.50, bf16[128,8,128]{0,2,1:T(8,128)(2,1)S(1)} %bitcast.281, bf16[128,8,128]{0,2,1:T(8,128)(2,1)S(1)} %bitcast.269, f32[8,128]{1,0:T(8,128)S(1)} %fusion.72, f32[8,128,2048]{1,2,0:T(8,128)} %get-tuple-element.182, f32[8,128]{1,0:T(8,128)S(1)} %get-tuple-element.181, ...), kind=kOutput, calls=%fused_computation.80 | convolution fusion | flops 1084489728 | bytes 9969664 | tf_op jit(solution)/shard_map/while/body/eval_jaxpr/htk,thd->kd/dot_general | solution.py:50
  245.9 4.7 %fusion.54 = bf16[2048,1024]{0,1:T(8,128)(2,1)} fusion(bf16[2048,1024]{0,1:T(8,128)(2,1)} %fusion.52, bf16[8,128,2048]{1,2,0:T(8,128)(2,1)} %fusion.39, bf16[128,8,128]{0,2,1:T(8,128)(2,1)S(1)} %bitcast.279), kind=kOutput, calls=%fused_computation.82 | convolution fusion | flops 537133056 | bytes 4980736 | tf_op jit(solution)/shard_map/while/body/eval_jaxpr/htk,thd->kd/dot_general | solution.py:53
  250.6 2.3 fusion.56
  252.9 2.3 fusion.58
  255.2 2.3 fusion.60
  257.5 6.4 %copy.147 = bf16[2048,1024]{1,0:T(8,128)(2,1)} copy(bf16[2048,1024]{0,1:T(8,128)(2,1)} %fusion.60) | data formatting | bytes 8388608
  263.9 66.6 %reduce-scatter.4.cloned.1.call-done = bf16[128,1024]{1,0:T(8,128)(2,1)} async-done(((bf16[2048,1024]{1,0:T(8,128)(2,1)}), bf16[128,1024]{1,0:T(8,128)(2,1)}) %reduce-scatter.4.cloned.1.call-update) | async-done | bytes 262160
  330.5 3.8 %fusion.35 = f32[128,4096]{1,0:T(8,128)S(1)} fusion(bf16[4096,1024]{1,0:T(8,128)(2,1)} %bitcast.263, bf16[128,1024]{1,0:T(8,128)(2,1)} %reduce-scatter.4.cloned.1.call-done), kind=kOutput, calls=%fused_computation.52 | convolution fusion | flops 536870912 | bytes 6422528 | tf_op jit(solution)/shard_map/dot_general | solution.py:127
  334.3 3.8 %fusion.68 = (f32[128]{0:T(128)S(1)}, f32[128,4096]{1,0:T(8,128)S(1)}) fusion(bf16[1,128,4096]{2,1,0:T(8,128)(2,1)S(1)} %copy-done, f32[4096]{0:T(1024)S(1)} %copy-done.12, f32[128,4096]{1,0:T(8,128)S(1)} %fusion.35, bf16[4096,1024]{1,0:T(8,128)(2,1)} %bitcast.264, bf16[128,1024]{1,0:T(8,128)(2,1)S(1)} %copy-done.8), kind=kOutput, calls=%fused_computation.96 | convolution fusion | flops 539492224 | bytes 9585152 | tf_op jit(solution)/shard_map/dot_general | solution.py:129
  338.0 1.6 fusion.79
  (50 shorter events, 5.9 us)
Async XLA Ops:
  6.5 100.1 %all-gather.7.cloned.1.call-start = ((), (), s32[]{:S(2)}) async-start(), calls=%async_computation.2 | async-start | bytes 8912896 | tf_op jit(solution)/shard_map/all_gather | solution.py:70
  50.0 59.9 %copy-start = (bf16[1,128,4096]{2,1,0:T(8,128)(2,1)S(1)}, bf16[1,128,4096]{2,1,0:T(8,128)(2,1)}, u32[]{:S(2)}) copy-start(bf16[1,128,4096]{2,1,0:T(8,128)(2,1)} %param.8) | copy-start | bytes 3145732
  50.0 59.9 %copy-start.12 = (f32[4096]{0:T(1024)S(1)}, f32[4096]{0:T(1024)}, u32[]{:S(2)}) copy-start(f32[4096]{0:T(1024)} %param.9) | copy-start | bytes 49156
  50.0 104.4 %all-gather.5.cloned.1.call-start = ((), (), s32[]{:S(2)}) async-start(), calls=%async_computation.1 | async-start | bytes 4456448 | tf_op jit(solution)/shard_map/all_gather | solution.py:91
  109.9 3.9 %copy-start.13 = (s32[1,32]{1,0:T(1,128)S(1)}, s32[1,32]{1,0:T(1,128)}, u32[]{:S(2)}) copy-start(s32[1,32]{1,0:T(1,128)} %param.15) | copy-start | bytes 388
  109.9 4.0 %copy-start.14 = (s32[1,16]{1,0:T(1,128)S(1)}, s32[1,16]{1,0:T(1,128)}, u32[]{:S(2)}) copy-start(s32[1,16]{1,0:T(1,128)} %param.14) | copy-start | bytes 196
  109.9 4.3 %copy-start.7 = (bf16[1,128,4096]{2,1,0:T(8,128)(2,1)S(1)}, bf16[1,128,4096]{2,1,0:T(8,128)(2,1)}, u32[]{:S(2)}) copy-start(bf16[1,128,4096]{2,1,0:T(8,128)(2,1)} %param.12) | copy-start | bytes 3145732
  113.7 216.7 %reduce-scatter.4.cloned.1.call-start = ((), (), s32[]{:S(2)}) async-start(), calls=%async_computation.3 | async-start | bytes 4456448
  161.3 6.0 %copy-start.11 = (bf16[128,1024]{0,1:T(8,128)(2,1)S(1)}, bf16[128,1024]{0,1:T(8,128)(2,1)}, u32[]{:S(2)}) copy-start(bf16[128,1024]{0,1:T(8,128)(2,1)} %get-tuple-element.164) | copy-start | bytes 786436
  174.2 6.0 %copy-start.9 = (bf16[128,1024]{0,1:T(8,128)(2,1)S(1)}, bf16[128,1024]{0,1:T(8,128)(2,1)}, u32[]{:S(2)}) copy-start(bf16[128,1024]{0,1:T(8,128)(2,1)} %get-tuple-element.157) | copy-start | bytes 786436
  200.2 6.3 %copy-start.1 = (bf16[8,128,2048]{1,2,0:T(8,128)(2,1)S(1)}, bf16[8,128,2048]{1,2,0:T(8,128)(2,1)}, u32[]{:S(2)}) copy-start(bf16[8,128,2048]{1,2,0:T(8,128)(2,1)} %fusion.40) | copy-start | bytes 12582916
  206.4 2.4 copy-start.4
  218.0 3.6 %copy-start.5 = (bf16[8,128,2048]{1,2,0:T(8,128)(2,1)S(1)}, bf16[8,128,2048]{1,2,0:T(8,128)(2,1)}, u32[]{:S(2)}) copy-start(bf16[8,128,2048]{1,2,0:T(8,128)(2,1)} %fusion.42) | copy-start | bytes 12582916
  221.3 2.2 copy-start.10
  245.9 4.7 %copy-start.2 = (bf16[8,128,2048]{1,2,0:T(8,128)(2,1)S(1)}, bf16[8,128,2048]{1,2,0:T(8,128)(2,1)}, u32[]{:S(2)}) copy-start(bf16[8,128,2048]{1,2,0:T(8,128)(2,1)} %fusion.40) | copy-start | bytes 12582916
  250.6 2.3 copy-start.3
  252.9 2.3 copy-start.6
  330.5 3.8 %copy-start.8 = (bf16[128,1024]{1,0:T(8,128)(2,1)S(1)}, bf16[128,1024]{1,0:T(8,128)(2,1)}, u32[]{:S(2)}) copy-start(bf16[128,1024]{1,0:T(8,128)(2,1)} %reduce-scatter.4.cloned.1.call-done) | copy-start | bytes 786436
Sparse Core Ops, SparseCore 0:
  50.1 56.4 all-gather.6
  113.8 40.5 all-gather.4
  264.0 66.4 reduce-scatter.3

commit v3 on v2

v3 whole, which is shorter than its diff:
```python
import functools

import jax
import jax.numpy as jnp
from jax import lax
from jax.experimental import pallas as pl
from jax.experimental.pallas import tpu as pltpu
from jax.sharding import PartitionSpec as P

HEADS = 32
KV_HEADS = 4
HEAD = 128
DOC_BLOCK = 128


def attn_kernel(q_ref, do_ref, k_ref, v_ref, qpos_ref, qdoc_ref, kpos_ref, kdoc_ref,
                out_ref, kg_acc, vg_acc, *, group_size, score_scale):
    allowed = (kpos_ref[...] <= qpos_ref[...]) & (kdoc_ref[...] == qdoc_ref[...])
    key_block = k_ref[...]
    value_block = v_ref[...]
    kg_acc[...] = jnp.zeros_like(kg_acc)
    vg_acc[...] = jnp.zeros_like(vg_acc)
    nt = (((1,), (1,)), ((), ()))
    tn = (((0,), (0,)), ((), ()))

    def head_step(h, carry):
        col = pl.multiple_of(h * HEAD, HEAD)
        q_h = q_ref[:, pl.ds(col, HEAD)]
        do_h = do_ref[:, pl.ds(col, HEAD)]
        raw = lax.dot_general(q_h, key_block, nt, preferred_element_type=jnp.float32)
        scores = jnp.where(allowed, raw * score_scale, -jnp.inf)
        row_max = jnp.max(scores, axis=1, keepdims=True)
        raised = jnp.exp(scores - row_max)
        soft = raised / jnp.sum(raised, axis=1, keepdims=True)
        soft_half = soft.astype(jnp.bfloat16)
        attn = jnp.dot(soft_half, value_block, preferred_element_type=jnp.float32)
        delta = jnp.sum(attn * do_h.astype(jnp.float32), axis=1, keepdims=True)
        dprobs = lax.dot_general(do_h, value_block, nt, preferred_element_type=jnp.float32)
        grad = (soft * (dprobs - delta) * score_scale).astype(jnp.bfloat16)
        kg_acc[...] += lax.dot_general(grad, q_h, tn, preferred_element_type=jnp.float32)
        vg_acc[...] += lax.dot_general(soft_half, do_h, tn, preferred_element_type=jnp.float32)
        return carry

    lax.fori_loop(0, group_size, head_step, 0)
    out_ref[:, :HEAD] = kg_acc[...].astype(out_ref.dtype)
    out_ref[:, HEAD:] = vg_acc[...].astype(out_ref.dtype)


def attend_all(queries, d_out, all_kv, qpos, qdoc, kpos, kdoc, kv_heads):
    tok_rows, width = queries.shape
    seq_len = all_kv.shape[0]
    group_size = width // (kv_heads * HEAD)
    kern = functools.partial(attn_kernel, group_size=group_size, score_scale=HEAD ** (-0.5))
    gw = group_size * HEAD
    return pl.pallas_call(
        kern,
        grid=(kv_heads,),
        in_specs=[
            pl.BlockSpec((tok_rows, gw), lambda g: (0, g)),
            pl.BlockSpec((tok_rows, gw), lambda g: (0, g)),
            pl.BlockSpec((seq_len, HEAD), lambda g: (0, 2 * g)),
            pl.BlockSpec((seq_len, HEAD), lambda g: (0, 2 * g + 1)),
            pl.BlockSpec((tok_rows, 1), lambda g: (0, 0)),
            pl.BlockSpec((tok_rows, 1), lambda g: (0, 0)),
            pl.BlockSpec((1, seq_len), lambda g: (0, 0)),
            pl.BlockSpec((1, seq_len), lambda g: (0, 0)),
        ],
        out_specs=pl.BlockSpec((seq_len, 2 * HEAD), lambda g: (0, g)),
        out_shape=jax.ShapeDtypeStruct((seq_len, 2 * kv_heads * HEAD), jnp.bfloat16),
        scratch_shapes=[pltpu.VMEM((seq_len, HEAD), jnp.float32),
                        pltpu.VMEM((seq_len, HEAD), jnp.float32)],
    )(queries, d_out, all_kv, all_kv, qpos, qdoc, kpos, kdoc)


def gather_weights(local_w, ctx_ways):
    shard_rows = local_w.shape[0]
    piece_rows = shard_rows // ctx_ways
    start = lax.axis_index("ctx") * piece_rows
    piece = lax.dynamic_slice_in_dim(local_w, start, piece_rows, axis=0)
    by_shard = lax.all_gather(piece, "dp", axis=0, tiled=False)
    full = lax.all_gather(by_shard, "ctx", axis=1, tiled=False)
    return full.reshape(-1, local_w.shape[1])


def body(embeds, norm_gain, w_key, w_value, queries, d_out, block_doc, slot_order):
    embed_rows = embeds[0]
    tok_rows = embed_rows.shape[0]
    ctx_ways = lax.axis_size("ctx")
    seq_len = tok_rows * ctx_ways
    half_len = tok_rows // 2
    as_float = embed_rows.astype(jnp.float32)
    inv_rms = lax.rsqrt(jnp.mean(as_float * as_float, axis=-1, keepdims=True) + 1e-05)
    normed = (as_float * inv_rms * norm_gain).astype(jnp.bfloat16)
    shard_rows = w_key.shape[0]
    local_w = jnp.stack(
        [w_key.reshape(shard_rows, KV_HEADS, HEAD), w_value.reshape(shard_rows, KV_HEADS, HEAD)],
        axis=2,
    ).reshape(shard_rows, 2 * KV_HEADS * HEAD)
    weights = gather_weights(local_w, ctx_ways)
    local_kv = jnp.dot(normed, weights, preferred_element_type=jnp.float32).astype(jnp.bfloat16)
    all_kv = lax.all_gather(local_kv, "ctx", axis=0, tiled=True)
    row_ids = jnp.arange(seq_len, dtype=jnp.int32)
    slot_hit = (row_ids // half_len)[:, None] == jnp.arange(2 * ctx_ways, dtype=jnp.int32)[None, :]
    key_pos = (
        jnp.sum(jnp.where(slot_hit, slot_order[0][None, :], 0), axis=1) * half_len
        + row_ids % half_len
    )
    block_hit = (key_pos // DOC_BLOCK)[:, None] == jnp.arange(block_doc.shape[1], dtype=jnp.int32)[
        None, :
    ]
    key_doc = jnp.sum(jnp.where(block_hit, block_doc[0][None, :], 0), axis=1)
    row_start = lax.axis_index("ctx") * tok_rows
    query_pos = lax.dynamic_slice_in_dim(key_pos, row_start, tok_rows)
    query_doc = lax.dynamic_slice_in_dim(key_doc, row_start, tok_rows)
    grad_terms = attend_all(
        queries[0], d_out[0], all_kv, query_pos[:, None], query_doc[:, None],
        key_pos[None, :], key_doc[None, :], KV_HEADS,
    )
    own_sum = lax.psum_scatter(grad_terms, "ctx", scatter_dimension=0, tiled=True)
    contract = (((1,), (1,)), ((), ()))
    grad_normed = lax.dot_general(own_sum, weights, contract, preferred_element_type=jnp.float32)
    mean_term = jnp.mean(as_float * norm_gain * grad_normed, axis=-1, keepdims=True)
    grad_embed = (
        inv_rms * norm_gain * grad_normed - as_float * inv_rms * inv_rms * inv_rms * mean_term
    )
    return grad_embed.astype(jnp.bfloat16)[None]


def solution(mesh):
    in_specs = (
        P("dp", "ctx", None),
        P(),
        P("dp", None),
        P("dp", None),
        P("dp", "ctx", None),
        P("dp", "ctx", None),
        P("dp", None),
        P("dp", None),
    )
    out_specs = P("dp", "ctx", None)
    return jax.shard_map(body, mesh=mesh, in_specs=in_specs, out_specs=out_specs, check_vma=False)
```

time: 349 us -> 289 us (0.83)
  matrix products: 91.7 us -> 11.9 us
  Pallas kernels: 0 us -> 51.1 us
  other arithmetic: 30.8 us -> 2.81 us
  local copies, waits for them, and re-layouts: 10.6 us -> 4.09 us
  waiting for transfers between devices: 157 us -> 161 us
    reduce_scatter x0 -> x1, waiting for transfers between devices: none -> 66.6 us  [body(): lax.psum_scatter(grad_terms, 'ctx', scatter_dimension=0, tiled=True)]
    unnamed x4 -> x3, waiting for transfers between devices: 66.6 us -> 0.05 us
    pallas_call x0 -> x1, Pallas kernels: none -> 51.1 us  [attend_all(): pl.pallas_call(kern, grid=(kv_heads,), in_specs=[pl.BlockSpec((tok_rows,...]
    dot_general x12 -> x2, matrix products: 55.2 us -> 11.9 us  [the longest x1 6.46 us: body(): lax.dot_general(own_sum, weights, contract, preferred_element_type=jnp.fl...]
    sub x4 -> x0, matrix products: 27.6 us -> none  [attend(): raised = jnp.exp(scores - row_max[None, :, :, None])]
    convert_element_type x4 -> x0, other arithmetic: 24.4 us -> none  [attend(): probs_half = soft_probs.astype(jnp.bfloat16)]
    unnamed x4 -> x0, matrix products: 8.89 us -> none
    unnamed x33 -> x12, local copies, waits for them, and re-layouts: 9.46 us -> 2.27 us
  transfers between devices with their start and end apart: 3 -> 3, of which waited for: 3 -> 3; matrix products, arithmetic and copies ran while one was open for 2% -> 1% of each run, Pallas kernels for 0% -> 0%
where the time goes in v3:
time: 289 us; the launch traced here: 287 us
  waiting for transfers between devices  161 us (56%)
  Pallas kernels  51.1 us (18%)
  blocking collectives  42.7 us (15%)
  between operations  13.2 us (5%)
  matrix products  11.9 us (4%)
  local copies, waits for them, and re-layouts  4.09 us (1%)
    reduce_scatter x1, waiting for transfers between devices, body(): lax.psum_scatter(grad_terms, 'ctx', scatter_dimension=0, tiled=True)  66.6 us
    all_gather x1, waiting for transfers between devices, gather_weights(): full = lax.all_gather(by_shard, 'ctx', axis=1, tiled=False)  56.2 us
    pallas_call x1, Pallas kernels, attend_all(): pl.pallas_call(kern, grid=(kv_heads,), in_specs=[pl.BlockSpec((tok_rows,...  51.1 us
    all_gather x1, blocking collectives, gather_weights(): by_shard = lax.all_gather(piece, 'dp', axis=0, tiled=False)  42.7 us
    all_gather x1, waiting for transfers between devices, body(): all_kv = lax.all_gather(local_kv, 'ctx', axis=0, tiled=True)  38.2 us
    dot_general x1, matrix products, body(): lax.dot_general(own_sum, weights, contract, preferred_element_type=jnp.fl...  6.46 us
  transfers between devices with their start and end apart: 3, of which 3 were waited for; matrix products, arithmetic and copies ran while one was open for 1% of the time, Pallas kernels for 0%

profile of v3, /device:TPU:1, one launch (start us, length us, event | category | flops | bytes accessed | tf_op | source)
XLA Modules:
  0.0 287.0 jit_solution(14890619105851052130)
XLA Ops:
  6.5 0.0 all-gather.7.cloned.1.call-start
  6.5 1.2 copy.25
  7.7 1.1 copy.26
  8.8 0.0 copy-start.1
  8.8 0.1 pad_maximum_fusion
  8.9 0.1 constant_dynamic-slice_fusion
  9.0 0.1 copy.27
  9.1 42.7 %all-gather = bf16[256,1024]{1,0:T(8,128)(2,1)} all-gather(bf16[16,1024]{1,0:T(8,128)(2,1)S(1)} %copy.27), channel_id=2, replica_groups=mesh['dp'=16,'ctx'=16] {'dp'}, dimensions={0}, use_global_device_ids=true | all-gather | bytes 557056 | tf_op jit(solution)/shard_map/all_gather | solution.py:80
  51.8 0.0 all-gather.7.cloned.1.call-update
  51.9 0.0 all-gather.5.cloned.1.call-start
  51.9 0.0 copy-done
  51.9 0.3 fusion.3
  52.2 56.2 %all-gather.7.cloned.1.call-done = bf16[16,256,1024]{2,1,0:T(8,128)(2,1)} async-done(((bf16[16,16,1024]{2,1,0:T(8,128)(2,1)}), bf16[16,256,1024]{2,1,0:T(8,128)(2,1)}) %all-gather.7.cloned.1.call-update) | async-done | bytes 8388624 | tf_op jit(solution)/shard_map/all_gather | solution.py:81
  108.5 0.0 copy-done.1
  108.5 5.4 %convolution_convert_fusion = bf16[128,1024]{1,0:T(8,128)(2,1)} fusion(bf16[4096,1024]{1,0:T(8,128)(2,1)} %bitcast.49, bf16[1,128,4096]{2,1,0:T(8,128)(2,1)S(1)} %copy-done, f32[4096]{0:T(1024)S(1)} %copy-done.1, f32[128]{0:T(128)S(1)} %add_rsqrt_fusion), kind=kOutput, calls=%fused_computation.15 | convolution fusion | flops 1075970048 | bytes 9716224 | tf_op jit(solution)/shard_map/dot_general | solution.py:100
  113.9 0.0 all-gather.5.cloned.1.call-update
  113.9 0.0 reduce-scatter.2.cloned.1.call-start
  114.0 0.0 copy-done.3
  114.0 0.1 select_reduce_fusion
  114.1 0.0 copy-done.4
  114.1 0.1 select_reduce_fusion.1
  114.2 0.1 dynamic-slice_bitcast_fusion
  114.3 0.8 copy.29.qdoc_ref
  115.1 0.7 copy.28.qpos_ref
  115.8 0.6 fusion.24.kpos_ref
  116.4 38.2 %all-gather.5.cloned.1.call-done.k_ref.v_ref = bf16[2048,1024]{1,0:T(8,128)(2,1)} async-done(((bf16[128,1024]{1,0:T(8,128)(2,1)}), bf16[2048,1024]{1,0:T(8,128)(2,1)}) %all-gather.5.cloned.1.call-update) | async-done | bytes 4194320 | tf_op jit(solution)/shard_map/all_gather | solution.py:101
  154.7 0.0 copy-done.2
  154.7 51.1 %shard_map.82 = bf16[2048,1024]{1,0:T(8,128)(2,1)} custom-call(bf16[128,4096]{1,0:T(8,128)(2,1)} %bitcast.53, bf16[128,4096]{1,0:T(8,128)(2,1)} %bitcast.54, bf16[2048,1024]{1,0:T(8,128)(2,1)} %all-gather.5.cloned.1.call-done.k_ref.v_ref, bf16[2048,1024]{1,0:T(8,128)(2,1)} %all-gather.5.cloned.1.call-done.k_ref.v_ref, s32[128,1]{1,0:T(8,128)} %copy.28.qpos_ref, ...), custom_call_target="tpu_custom_call" | custom-call | tf_op jit(solution)/shard_map/pallas_call | solution.py:55
  205.7 0.0 reduce-scatter.2.cloned.1.call-update
  205.8 66.6 %reduce-scatter.2.cloned.1.call-done = bf16[128,1024]{1,0:T(8,128)(2,1)} async-done(((bf16[2048,1024]{1,0:T(8,128)(2,1)}), bf16[128,1024]{1,0:T(8,128)(2,1)}) %reduce-scatter.2.cloned.1.call-update) | async-done | bytes 262160 | tf_op jit(solution)/shard_map/reduce_scatter | solution.py:119
  272.3 6.5 %fusion.10 = (f32[128]{0:T(128)S(1)}, f32[128,4096]{1,0:T(8,128)S(1)}) fusion(bf16[1,128,4096]{2,1,0:T(8,128)(2,1)S(1)} %copy-done, f32[4096]{0:T(1024)S(1)} %copy-done.1, bf16[128,1024]{1,0:T(8,128)(2,1)} %reduce-scatter.2.cloned.1.call-done, bf16[4096,1024]{1,0:T(8,128)(2,1)} %bitcast.50), kind=kOutput, calls=%fused_computation.12 | convolution fusion | flops 1075838848 | bytes 11813376 | tf_op jit(solution)/shard_map/dot_general | solution.py:121
  278.8 1.6 fusion.15
  (8 shorter events, 0.0 us)
Async XLA Ops:
  6.5 45.4 %copy-start = (bf16[1,128,4096]{2,1,0:T(8,128)(2,1)S(1)}, bf16[1,128,4096]{2,1,0:T(8,128)(2,1)}, u32[]{:S(2)}) copy-start(bf16[1,128,4096]{2,1,0:T(8,128)(2,1)} %param.8) | copy-start | bytes 3145732
  6.5 101.9 %all-gather.7.cloned.1.call-start = ((), (), s32[]{:S(2)}) async-start(), calls=%async_computation.3 | async-start | bytes 8912896 | tf_op jit(solution)/shard_map/all_gather | solution.py:81
  8.8 99.7 %copy-start.1 = (f32[4096]{0:T(1024)S(1)}, f32[4096]{0:T(1024)}, u32[]{:S(2)}) copy-start(f32[4096]{0:T(1024)} %param.9) | copy-start | bytes 49156
  51.9 102.8 %all-gather.5.cloned.1.call-start = ((), (), s32[]{:S(2)}) async-start(), calls=%async_computation.1 | async-start | bytes 4456448 | tf_op jit(solution)/shard_map/all_gather | solution.py:101
  108.5 5.5 %copy-start.3 = (s32[1,32]{1,0:T(1,128)S(1)}, s32[1,32]{1,0:T(1,128)}, u32[]{:S(2)}) copy-start(s32[1,32]{1,0:T(1,128)} %param.15) | copy-start | bytes 388
  108.5 5.7 %copy-start.4 = (s32[1,16]{1,0:T(1,128)S(1)}, s32[1,16]{1,0:T(1,128)}, u32[]{:S(2)}) copy-start(s32[1,16]{1,0:T(1,128)} %param.14) | copy-start | bytes 196
  113.9 158.4 %reduce-scatter.2.cloned.1.call-start = ((), (), s32[]{:S(2)}) async-start(), calls=%async_computation.2 | async-start | bytes 4456448 | tf_op jit(solution)/shard_map/reduce_scatter | solution.py:119
  114.2 40.4 %copy-start.2 = (s32[2048]{0:T(1024)}, s32[2048]{0:T(1024)S(1)}, u32[]{:S(2)}) copy-start(s32[2048]{0:T(1024)S(1)} %select_reduce_fusion.1) | copy-start | bytes 24580
Sparse Core Ops, SparseCore 0:
  52.0 56.4 all-gather.6
  114.0 40.5 all-gather.4
  205.9 66.4 reduce-scatter.1

commit v4 on v3

--- a/solution.py
+++ b/solution.py
@@ -5,7 +5,7 @@
 from jax import lax
 from jax.experimental import pallas as pl
 from jax.experimental.pallas import tpu as pltpu
-from jax.sharding import PartitionSpec as P
+from jax.sharding import Mesh, PartitionSpec as P
 
 HEADS = 32
 KV_HEADS = 4
@@ -72,20 +72,37 @@
     )(queries, d_out, all_kv, all_kv, qpos, qdoc, kpos, kdoc)
 
 
+CTX = ("chip", "core")
+
+
 def gather_weights(local_w, ctx_ways):
+    dp_ways = lax.axis_size("dp")
     shard_rows = local_w.shape[0]
     piece_rows = shard_rows // ctx_ways
-    start = lax.axis_index("ctx") * piece_rows
+    start = lax.axis_index(CTX) * piece_rows
     piece = lax.dynamic_slice_in_dim(local_w, start, piece_rows, axis=0)
-    by_shard = lax.all_gather(piece, "dp", axis=0, tiled=False)
-    full = lax.all_gather(by_shard, "ctx", axis=1, tiled=False)
+    spread = jnp.broadcast_to(piece[None], (dp_ways,) + piece.shape)
+    by_shard = lax.all_to_all(spread, "dp", 0, 0, tiled=False)
+    full = lax.all_gather(by_shard, CTX, axis=1, tiled=False)
     return full.reshape(-1, local_w.shape[1])
+
+
+def scatter_sum(terms, tok_rows):
+    core_ways = lax.axis_size("core")
+    chip_ways = lax.axis_size("chip")
+    width = terms.shape[1]
+    mine = lax.all_to_all(
+        terms.reshape(chip_ways, core_ways, tok_rows, width), "core", 1, 1, tiled=False
+    )
+    mine = jnp.sum(mine.astype(jnp.float32), axis=1).astype(jnp.bfloat16)
+    mine = lax.all_to_all(mine, "chip", 0, 0, tiled=False)
+    return jnp.sum(mine.astype(jnp.float32), axis=0).astype(jnp.bfloat16)
 
 
 def body(embeds, norm_gain, w_key, w_value, queries, d_out, block_doc, slot_order):
     embed_rows = embeds[0]
     tok_rows = embed_rows.shape[0]
-    ctx_ways = lax.axis_size("ctx")
+    ctx_ways = lax.axis_size(CTX)
     seq_len = tok_rows * ctx_ways
     half_len = tok_rows // 2
     as_float = embed_rows.astype(jnp.float32)
@@ -98,7 +115,7 @@
     ).reshape(shard_rows, 2 * KV_HEADS * HEAD)
     weights = gather_weights(local_w, ctx_ways)
     local_kv = jnp.dot(normed, weights, preferred_element_type=jnp.float32).astype(jnp.bfloat16)
-    all_kv = lax.all_gather(local_kv, "ctx", axis=0, tiled=True)
+    all_kv = lax.all_gather(local_kv, CTX, axis=0, tiled=True)
     row_ids = jnp.arange(seq_len, dtype=jnp.int32)
     slot_hit = (row_ids // half_len)[:, None] == jnp.arange(2 * ctx_ways, dtype=jnp.int32)[None, :]
     key_pos = (
@@ -109,14 +126,14 @@
         None, :
     ]
     key_doc = jnp.sum(jnp.where(block_hit, block_doc[0][None, :], 0), axis=1)
-    row_start = lax.axis_index("ctx") * tok_rows
+    row_start = lax.axis_index(CTX) * tok_rows
     query_pos = lax.dynamic_slice_in_dim(key_pos, row_start, tok_rows)
     query_doc = lax.dynamic_slice_in_dim(key_doc, row_start, tok_rows)
     grad_terms = attend_all(
         queries[0], d_out[0], all_kv, query_pos[:, None], query_doc[:, None],
         key_pos[None, :], key_doc[None, :], KV_HEADS,
     )
-    own_sum = lax.psum_scatter(grad_terms, "ctx", scatter_dimension=0, tiled=True)
+    own_sum = scatter_sum(grad_terms, tok_rows)
     contract = (((1,), (1,)), ((), ()))
     grad_normed = lax.dot_general(own_sum, weights, contract, preferred_element_type=jnp.float32)
     mean_term = jnp.mean(as_float * norm_gain * grad_normed, axis=-1, keepdims=True)
@@ -127,15 +144,17 @@
 
 
 def solution(mesh):
+    dp_ways, ctx_ways = mesh.shape["dp"], mesh.shape["ctx"]
+    fine = Mesh(mesh.devices.reshape(dp_ways, ctx_ways // 2, 2), ("dp",) + CTX)
     in_specs = (
-        P("dp", "ctx", None),
+        P("dp", CTX, None),
         P(),
         P("dp", None),
         P("dp", None),
-        P("dp", "ctx", None),
-        P("dp", "ctx", None),
+        P("dp", CTX, None),
+        P("dp", CTX, None),
         P("dp", None),
         P("dp", None),
     )
-    out_specs = P("dp", "ctx", None)
-    return jax.shard_map(body, mesh=mesh, in_specs=in_specs, out_specs=out_specs, check_vma=False)
+    out_specs = P("dp", CTX, None)
+    return jax.shard_map(body, mesh=fine, in_specs=in_specs, out_specs=out_specs, check_vma=False)

time: 289 us -> 249 us (0.86)
  waiting for transfers between devices: 161 us -> 91.7 us
  blocking collectives: 42.7 us -> 65.2 us
  other arithmetic: 2.81 us -> 8.28 us
    reduce_scatter x1 -> x0, waiting for transfers between devices: 66.6 us -> none  [body(): lax.psum_scatter(grad_terms, 'ctx', scatter_dimension=0, tiled=True)]
    all_to_all x0 -> x3, blocking collectives: none -> 65.2 us  [the longest x1 30.1 us: scatter_sum(): mine = lax.all_to_all(mine, 'chip', 0, 0, tiled=False)]
    all_gather x1 -> x0, blocking collectives: 42.7 us -> none  [gather_weights(): by_shard = lax.all_gather(piece, 'dp', axis=0, tiled=False)]
    reduce_sum x0 -> x2, other arithmetic: none -> 5.47 us  [the longest x1 3.51 us: scatter_sum(): mine = jnp.sum(mine.astype(jnp.float32), axis=1).astype(jnp.bfloat16)]
  transfers between devices with their start and end apart: 3 -> 2, of which waited for: 3 -> 2; matrix products, arithmetic and copies ran while one was open for 1% -> 1% of each run, Pallas kernels for 0% -> 0%
where the time goes in v4:
time: 249 us; the launch traced here: 248 us
  waiting for transfers between devices  91.7 us (37%)
  blocking collectives  65.2 us (26%)
  Pallas kernels  51 us (20%)
  between operations  13.5 us (5%)
  matrix products  11.8 us (5%)
  other arithmetic  8.28 us (3%)
  local copies, waits for them, and re-layouts  6.67 us (3%)
    all_gather x1, waiting for transfers between devices, gather_weights(): full = lax.all_gather(by_shard, CTX, axis=1, tiled=False)  53.3 us
    pallas_call x1, Pallas kernels, attend_all(): pl.pallas_call(kern, grid=(kv_heads,), in_specs=[pl.BlockSpec((tok_rows,...  51 us
    all_gather x1, waiting for transfers between devices, body(): all_kv = lax.all_gather(local_kv, CTX, axis=0, tiled=True)  38.3 us
    all_to_all x1, blocking collectives, scatter_sum(): mine = lax.all_to_all(mine, 'chip', 0, 0, tiled=False)  30.1 us
    all_to_all x1, blocking collectives, gather_weights(): by_shard = lax.all_to_all(spread, 'dp', 0, 0, tiled=False)  26.9 us
    all_to_all x1, blocking collectives, scatter_sum(): lax.all_to_all(terms.reshape(chip_ways, core_ways, tok_rows, width), 'cor...  8.15 us
    dot_general x1, matrix products, body(): lax.dot_general(own_sum, weights, contract, preferred_element_type=jnp.fl...  6.36 us
    dot_general x1, matrix products, body(): jnp.dot(normed, weights, preferred_element_type=jnp.float32)  5.41 us
  transfers between devices with their start and end apart: 2, of which 2 were waited for; matrix products, arithmetic and copies ran while one was open for 1% of the time, Pallas kernels for 0%

profile of v4, /device:TPU:1, one launch (start us, length us, event | category | flops | bytes accessed | tf_op | source)
XLA Modules:
  0.0 248.2 jit_solution(16189277756060579677)
XLA Ops:
  6.5 1.1 copy.22
  7.6 1.1 copy.23
  8.7 0.0 copy-start
  8.7 0.1 pad_maximum_fusion
  8.8 0.0 copy-start.1
  8.8 0.1 constant_dynamic-slice_fusion
  9.0 0.1 copy.24
  9.1 0.1 broadcast_in_dim.56
  9.1 26.9 %all_to_all.15 = bf16[16,16,1024]{2,1,0:T(8,128)(2,1)} all-to-all(bf16[16,16,1024]{2,1,0:T(8,128)(2,1)S(1)} %broadcast_in_dim.56), channel_id=1, replica_groups=mesh['dp'=16,'chip'=8,'core'=2] {'dp'}, dimensions={0} | all-to-all | bytes 1048576 | tf_op jit(solution)/shard_map/all_to_all | solution.py:85
  36.1 0.0 all-gather.6.cloned.1.call-update
  36.1 0.0 all-gather.4.cloned.1.call-start
  36.2 0.3 fusion.3
  36.5 53.3 %all-gather.6.cloned.1.call-done = bf16[16,256,1024]{2,1,0:T(8,128)(2,1)} async-done(((bf16[16,16,1024]{2,1,0:T(8,128)(2,1)}), bf16[16,256,1024]{2,1,0:T(8,128)(2,1)}) %all-gather.6.cloned.1.call-update) | async-done | bytes 8388624 | tf_op jit(solution)/shard_map/all_gather | solution.py:86
  89.8 5.4 %convolution_convert_fusion = bf16[128,1024]{1,0:T(8,128)(2,1)} fusion(bf16[4096,1024]{1,0:T(8,128)(2,1)} %bitcast.50, bf16[1,128,4096]{2,1,0:T(8,128)(2,1)S(1)} %copy-done, f32[4096]{0:T(1024)S(1)} %copy-done.1, f32[128]{0:T(128)S(1)} %add_rsqrt_fusion), kind=kOutput, calls=%fused_computation.15 | convolution fusion | flops 1075970048 | bytes 9716224 | tf_op jit(solution)/shard_map/dot_general | solution.py:117
  95.2 0.0 all-gather.4.cloned.1.call-update
  95.2 0.0 copy-done.3
  95.2 0.1 select_reduce_fusion
  95.4 0.1 select_reduce_fusion.1
  95.5 0.1 dynamic-slice_bitcast_fusion
  95.6 0.7 copy.26.qdoc_ref
  96.3 0.7 copy.25.qpos_ref
  97.0 0.6 fusion.24.kpos_ref
  97.6 38.3 %all-gather.4.cloned.1.call-done.k_ref.v_ref = bf16[2048,1024]{1,0:T(8,128)(2,1)} async-done(((bf16[128,1024]{1,0:T(8,128)(2,1)}), bf16[2048,1024]{1,0:T(8,128)(2,1)}) %all-gather.4.cloned.1.call-update) | async-done | bytes 4194320 | tf_op jit(solution)/shard_map/all_gather | solution.py:118
  135.9 0.0 copy-done.2
  135.9 51.0 %shard_map.82 = bf16[2048,1024]{1,0:T(8,128)(2,1)} custom-call(bf16[128,4096]{1,0:T(8,128)(2,1)} %bitcast.53, bf16[128,4096]{1,0:T(8,128)(2,1)} %bitcast.54, bf16[2048,1024]{1,0:T(8,128)(2,1)} %all-gather.4.cloned.1.call-done.k_ref.v_ref, bf16[2048,1024]{1,0:T(8,128)(2,1)} %all-gather.4.cloned.1.call-done.k_ref.v_ref, s32[128,1]{1,0:T(8,128)} %copy.25.qpos_ref, ...), custom_call_target="tpu_custom_call" | custom-call | tf_op jit(solution)/shard_map/pallas_call | solution.py:55
  187.0 2.6 %copy.27 = bf16[8,2,128,1024]{3,2,0,1:T(8,128)(2,1)S(1)} copy(bf16[8,2,128,1024]{3,2,1,0:T(8,128)(2,1)} %bitcast.49) | data formatting | bytes 8388608 | tf_op jit(solution)/shard_map/reshape | solution.py:95
  189.6 8.2 %all_to_all.16 = bf16[8,2,128,1024]{3,2,0,1:T(8,128)(2,1)} all-to-all(bf16[8,2,128,1024]{3,2,0,1:T(8,128)(2,1)S(1)} %copy.27), channel_id=1, replica_groups=mesh['dp'=16,'chip'=8,'core'=2] {'core'}, dimensions={1} | all-to-all | bytes 8388608 | tf_op jit(solution)/shard_map/all_to_all | solution.py:94
  197.8 3.5 %reduce_sum.63 = bf16[8,128,1024]{2,1,0:T(8,128)(2,1)S(1)} reduce(bf16[8,2,128,1024]{3,2,0,1:T(8,128)(2,1)} %all_to_all.16, bf16[]{:T(256)} %constant.77.clone.1), dimensions={1}, to_apply=%region_3.4 | reduce | flops 1048576 | bytes 6291458 | tf_op jit(solution)/shard_map/reduce_sum | solution.py:97
  201.3 30.1 %all_to_all.17 = bf16[8,128,1024]{2,1,0:T(8,128)(2,1)} all-to-all(bf16[8,128,1024]{2,1,0:T(8,128)(2,1)S(1)} %reduce_sum.63), channel_id=1, replica_groups=mesh['dp'=16,'chip'=8,'core'=2] {'chip'}, dimensions={0} | all-to-all | bytes 4194304 | tf_op jit(solution)/shard_map/all_to_all | solution.py:98
  231.4 2.0 reduce_sum.64
  233.3 6.4 %fusion.10 = (f32[128]{0:T(128)S(1)}, f32[128,4096]{1,0:T(8,128)S(1)}) fusion(bf16[1,128,4096]{2,1,0:T(8,128)(2,1)S(1)} %copy-done, f32[4096]{0:T(1024)S(1)} %copy-done.1, bf16[128,1024]{1,0:T(8,128)(2,1)S(1)} %reduce_sum.64, bf16[4096,1024]{1,0:T(8,128)(2,1)} %bitcast.51), kind=kOutput, calls=%fused_computation.12 | convolution fusion | flops 1075838848 | bytes 11813376 | tf_op jit(solution)/shard_map/dot_general | solution.py:138
  239.7 1.6 fusion.15
  (11 shorter events, 0.0 us)
Async XLA Ops:
  6.5 83.2 %all-gather.6.cloned.1.call-start = ((), (), s32[]{:S(2)}) async-start(), calls=%async_computation.4 | async-start | bytes 8912896 | tf_op jit(solution)/shard_map/all_gather | solution.py:86
  8.7 27.4 %copy-start = (bf16[1,128,4096]{2,1,0:T(8,128)(2,1)S(1)}, bf16[1,128,4096]{2,1,0:T(8,128)(2,1)}, u32[]{:S(2)}) copy-start(bf16[1,128,4096]{2,1,0:T(8,128)(2,1)} %param.8) | copy-start | bytes 3145732
  8.8 81.0 %copy-start.1 = (f32[4096]{0:T(1024)S(1)}, f32[4096]{0:T(1024)}, u32[]{:S(2)}) copy-start(f32[4096]{0:T(1024)} %param.9) | copy-start | bytes 49156
  36.1 99.8 %all-gather.4.cloned.1.call-start = ((), (), s32[]{:S(2)}) async-start(), calls=%async_computation.3 | async-start | bytes 4456448 | tf_op jit(solution)/shard_map/all_gather | solution.py:118
  89.8 5.5 %copy-start.3 = (s32[1,32]{1,0:T(1,128)S(1)}, s32[1,32]{1,0:T(1,128)}, u32[]{:S(2)}) copy-start(s32[1,32]{1,0:T(1,128)} %param.15) | copy-start | bytes 388
  89.8 5.6 %copy-start.4 = (s32[1,16]{1,0:T(1,128)S(1)}, s32[1,16]{1,0:T(1,128)}, u32[]{:S(2)}) copy-start(s32[1,16]{1,0:T(1,128)} %param.14) | copy-start | bytes 196
  95.5 40.5 %copy-start.2 = (s32[2048]{0:T(1024)}, s32[2048]{0:T(1024)S(1)}, u32[]{:S(2)}) copy-start(s32[2048]{0:T(1024)S(1)} %select_reduce_fusion.1) | copy-start | bytes 24580
Sparse Core Ops, SparseCore 0:
  36.2 53.4 all-gather.5
  95.3 40.5 all-gather.3

commit v5 on v4

--- a/solution.py
+++ b/solution.py
@@ -77,14 +77,22 @@
 
 def gather_weights(local_w, ctx_ways):
     dp_ways = lax.axis_size("dp")
+    chip_ways = lax.axis_size("chip")
     shard_rows = local_w.shape[0]
     piece_rows = shard_rows // ctx_ways
-    start = lax.axis_index(CTX) * piece_rows
+    start = (lax.axis_index("core") * chip_ways + lax.axis_index("chip")) * piece_rows
     piece = lax.dynamic_slice_in_dim(local_w, start, piece_rows, axis=0)
     spread = jnp.broadcast_to(piece[None], (dp_ways,) + piece.shape)
     by_shard = lax.all_to_all(spread, "dp", 0, 0, tiled=False)
-    full = lax.all_gather(by_shard, CTX, axis=1, tiled=False)
+    by_chip = lax.all_gather(by_shard, "chip", axis=1, tiled=False)
+    full = lax.all_gather(by_chip, "core", axis=1, tiled=False)
     return full.reshape(-1, local_w.shape[1])
+
+
+def gather_rows(local_rows):
+    by_chip = lax.all_gather(local_rows, "chip", axis=0, tiled=False)
+    full = lax.all_gather(by_chip, "core", axis=0, tiled=False)
+    return full.reshape(-1, local_rows.shape[1])
 
 
 def scatter_sum(terms, tok_rows):
@@ -92,9 +100,9 @@
     chip_ways = lax.axis_size("chip")
     width = terms.shape[1]
     mine = lax.all_to_all(
-        terms.reshape(chip_ways, core_ways, tok_rows, width), "core", 1, 1, tiled=False
+        terms.reshape(core_ways, chip_ways, tok_rows, width), "core", 0, 0, tiled=False
     )
-    mine = jnp.sum(mine.astype(jnp.float32), axis=1).astype(jnp.bfloat16)
+    mine = jnp.sum(mine.astype(jnp.float32), axis=0).astype(jnp.bfloat16)
     mine = lax.all_to_all(mine, "chip", 0, 0, tiled=False)
     return jnp.sum(mine.astype(jnp.float32), axis=0).astype(jnp.bfloat16)
 
@@ -115,7 +123,7 @@
     ).reshape(shard_rows, 2 * KV_HEADS * HEAD)
     weights = gather_weights(local_w, ctx_ways)
     local_kv = jnp.dot(normed, weights, preferred_element_type=jnp.float32).astype(jnp.bfloat16)
-    all_kv = lax.all_gather(local_kv, CTX, axis=0, tiled=True)
+    all_kv = gather_rows(local_kv)
     row_ids = jnp.arange(seq_len, dtype=jnp.int32)
     slot_hit = (row_ids // half_len)[:, None] == jnp.arange(2 * ctx_ways, dtype=jnp.int32)[None, :]
     key_pos = (
@@ -129,9 +137,15 @@
     row_start = lax.axis_index(CTX) * tok_rows
     query_pos = lax.dynamic_slice_in_dim(key_pos, row_start, tok_rows)
     query_doc = lax.dynamic_slice_in_dim(key_doc, row_start, tok_rows)
+    chip_ways = lax.axis_size("chip")
+    core_ways = lax.axis_size("core")
+
+    def gathered_order(per_row):
+        return per_row.reshape(chip_ways, core_ways, tok_rows).transpose(1, 0, 2).reshape(1, -1)
+
     grad_terms = attend_all(
         queries[0], d_out[0], all_kv, query_pos[:, None], query_doc[:, None],
-        key_pos[None, :], key_doc[None, :], KV_HEADS,
+        gathered_order(key_pos), gathered_order(key_doc), KV_HEADS,
     )
     own_sum = scatter_sum(grad_terms, tok_rows)
     contract = (((1,), (1,)), ((), ()))

time: 249 us -> 302 us (1.21)
  waiting for transfers between devices: 91.7 us -> 141 us
  blocking collectives: 65.2 us -> 69.8 us
    all_gather x2 -> x4, waiting for transfers between devices: 91.6 us -> 141 us  [the longest x1 53.5 us: gather_weights(): by_chip = lax.all_gather(by_shard, 'chip', axis=1, tiled=False)]
    all_to_all x1, blocking collectives: 8.15 us -> 11.7 us  [scatter_sum(): lax.all_to_all(terms.reshape(core_ways, chip_ways, tok_rows, width), 'cor...]
  transfers between devices with their start and end apart: 2 -> 4, of which waited for: 2 -> 4; matrix products, arithmetic and copies ran while one was open for 1% -> 1% of each run, Pallas kernels for 0% -> 0%
where the time goes in v5:
time: 302 us; the launch traced here: 301 us
  waiting for transfers between devices  141 us (47%)
  blocking collectives  69.8 us (23%)
  Pallas kernels  51 us (17%)
  between operations  13.2 us (4%)
  matrix products  11.7 us (4%)
  other arithmetic  7.7 us (3%)
  local copies, waits for them, and re-layouts  6.38 us (2%)
    all_gather x1, waiting for transfers between devices, gather_weights(): by_chip = lax.all_gather(by_shard, 'chip', axis=1, tiled=False)  53.5 us
    pallas_call x1, Pallas kernels, attend_all(): pl.pallas_call(kern, grid=(kv_heads,), in_specs=[pl.BlockSpec((tok_rows,...  51 us
    all_gather x1, waiting for transfers between devices, gather_rows(): by_chip = lax.all_gather(local_rows, 'chip', axis=0, tiled=False)  39.1 us
    all_to_all x1, blocking collectives, scatter_sum(): mine = lax.all_to_all(mine, 'chip', 0, 0, tiled=False)  31.2 us
    all_to_all x1, blocking collectives, gather_weights(): by_shard = lax.all_to_all(spread, 'dp', 0, 0, tiled=False)  26.9 us
    all_gather x1, waiting for transfers between devices, gather_weights(): full = lax.all_gather(by_chip, 'core', axis=1, tiled=False)  25.2 us
    all_gather x1, waiting for transfers between devices, gather_rows(): full = lax.all_gather(by_chip, 'core', axis=0, tiled=False)  23.1 us
    all_to_all x1, blocking collectives, scatter_sum(): lax.all_to_all(terms.reshape(core_ways, chip_ways, tok_rows, width), 'cor...  11.7 us
  transfers between devices with their start and end apart: 4, of which 4 were waited for; matrix products, arithmetic and copies ran while one was open for 1% of the time, Pallas kernels for 0%

profile of v5, /device:TPU:1, one launch (start us, length us, event | category | flops | bytes accessed | tf_op | source)
XLA Modules:
  0.0 301.0 jit_solution(9511520780479513261)
XLA Ops:
  6.5 1.1 copy.25
  7.6 1.1 copy.26
  8.7 0.1 pad_maximum_fusion
  8.8 0.1 constant_dynamic-slice_fusion
  8.9 0.1 copy.27
  9.0 0.1 broadcast_in_dim.52
  9.1 26.9 %all_to_all.15 = bf16[16,16,1024]{2,1,0:T(8,128)(2,1)} all-to-all(bf16[16,16,1024]{2,1,0:T(8,128)(2,1)S(1)} %broadcast_in_dim.52), channel_id=1, replica_groups=mesh['dp'=16,'chip'=8,'core'=2] {'dp'}, dimensions={0} | all-to-all | bytes 1048576 | tf_op jit(solution)/shard_map/all_to_all | solution.py:86
  36.0 0.0 all-gather.9.cloned.1.call-update
  36.1 0.0 all-gather.11.cloned.1.call-start
  36.1 53.5 %all-gather.9.cloned.1.call-done = bf16[16,128,1024]{2,1,0:T(8,128)(2,1)} async-done(((bf16[16,16,1024]{2,1,0:T(8,128)(2,1)}), bf16[16,128,1024]{2,1,0:T(8,128)(2,1)}) %all-gather.9.cloned.1.call-update) | async-done | bytes 4194320 | tf_op jit(solution)/shard_map/all_gather | solution.py:87
  89.6 0.0 all-gather.13.cloned.1.call-start
  89.7 1.1 copy-done
  90.8 0.3 fusion.3
  91.1 25.2 %all-gather.11.cloned.1.call-done = bf16[16,16,16,1024]{3,2,1,0:T(8,128)(2,1)} async-done(((bf16[16,8,16,1024]{3,2,1,0:T(8,128)(2,1)}), bf16[16,16,16,1024]{3,2,1,0:T(8,128)(2,1)}) %all-gather.11.cloned.1.call-update) | async-done | bytes 8388624 | tf_op jit(solution)/shard_map/all_gather | solution.py:88
  116.3 5.4 %convolution_convert_fusion = bf16[128,1024]{1,0:T(8,128)(2,1)} fusion(bf16[4096,1024]{1,0:T(8,128)(2,1)} %bitcast.61, bf16[1,128,4096]{2,1,0:T(8,128)(2,1)S(1)} %copy-done, f32[4096]{0:T(1024)S(1)} %copy-done.1, f32[128]{0:T(128)S(1)} %add_rsqrt_fusion), kind=kOutput, calls=%fused_computation.15 | convolution fusion | flops 1075970048 | bytes 9716224 | tf_op jit(solution)/shard_map/dot_general | solution.py:125
  121.8 0.0 all-gather.15.cloned.1.call-start
  121.8 39.1 %all-gather.13.cloned.1.call-done = bf16[1024,1024]{1,0:T(8,128)(2,1)} async-done(((bf16[128,1024]{1,0:T(8,128)(2,1)}), bf16[1024,1024]{1,0:T(8,128)(2,1)}) %all-gather.13.cloned.1.call-update) | async-done | bytes 2097168 | tf_op jit(solution)/shard_map/all_gather | solution.py:93
  161.0 0.1 select_reduce_fusion
  161.1 0.6 copy.28
  161.7 0.1 select_reduce_fusion.1
  161.8 0.6 copy.29
  162.4 0.1 dynamic-slice_bitcast_fusion
  162.5 0.7 copy.31.qdoc_ref
  163.2 0.7 copy.30.qpos_ref
  164.0 23.1 %all-gather.15.cloned.1.call-done = bf16[16,128,1024]{2,1,0:T(8,128)(2,1)} async-done(((bf16[8,128,1024]{2,1,0:T(8,128)(2,1)}), bf16[16,128,1024]{2,1,0:T(8,128)(2,1)}) %all-gather.15.cloned.1.call-update) | async-done | bytes 4194320 | tf_op jit(solution)/shard_map/all_gather | solution.py:94
  187.1 51.0 %shard_map.82 = bf16[2048,1024]{1,0:T(8,128)(2,1)} custom-call(bf16[128,4096]{1,0:T(8,128)(2,1)} %bitcast.66, bf16[128,4096]{1,0:T(8,128)(2,1)} %bitcast.67, bf16[2048,1024]{1,0:T(8,128)(2,1)} %bitcast.58, bf16[2048,1024]{1,0:T(8,128)(2,1)} %bitcast.59, s32[128,1]{1,0:T(8,128)} %copy.30.qpos_ref, s32[128,1]{1,0:T(8,128)} %copy.31.qdoc_ref, ...), custom_call_target="tpu_custom_call" | custom-call | tf_op jit(solution)/shard_map/pallas_call | solution.py:55
  238.1 11.7 %all_to_all.16 = bf16[2,8,128,1024]{3,2,1,0:T(8,128)(2,1)} all-to-all(bf16[2,8,128,1024]{3,2,1,0:T(8,128)(2,1)} %bitcast.60), channel_id=1, replica_groups=mesh['dp'=16,'chip'=8,'core'=2] {'core'}, dimensions={0} | all-to-all | bytes 8388608 | tf_op jit(solution)/shard_map/all_to_all | solution.py:102
  249.8 3.5 %reduce_sum.63 = bf16[8,128,1024]{2,1,0:T(8,128)(2,1)S(1)} reduce(bf16[2,8,128,1024]{3,2,1,0:T(8,128)(2,1)} %all_to_all.16, bf16[]{:T(256)} %constant.80.clone.1), dimensions={0}, to_apply=%region_3.4 | reduce | flops 1048576 | bytes 6291458 | tf_op jit(solution)/shard_map/reduce_sum | solution.py:105
  253.3 31.2 %all_to_all.17 = bf16[8,128,1024]{2,1,0:T(8,128)(2,1)} all-to-all(bf16[8,128,1024]{2,1,0:T(8,128)(2,1)S(1)} %reduce_sum.63), channel_id=1, replica_groups=mesh['dp'=16,'chip'=8,'core'=2] {'chip'}, dimensions={0} | all-to-all | bytes 4194304 | tf_op jit(solution)/shard_map/all_to_all | solution.py:106
  284.5 2.0 reduce_sum.64
  286.5 6.4 %fusion.10 = (f32[128]{0:T(128)S(1)}, f32[128,4096]{1,0:T(8,128)S(1)}) fusion(bf16[1,128,4096]{2,1,0:T(8,128)(2,1)S(1)} %copy-done, f32[4096]{0:T(1024)S(1)} %copy-done.1, bf16[128,1024]{1,0:T(8,128)(2,1)S(1)} %reduce_sum.64, bf16[4096,1024]{1,0:T(8,128)(2,1)} %bitcast.62), kind=kOutput, calls=%fused_computation.12 | convolution fusion | flops 1075838848 | bytes 11813376 | tf_op jit(solution)/shard_map/dot_general | solution.py:152
  292.9 1.6 fusion.15
  (16 shorter events, 0.1 us)
Async XLA Ops:
  6.5 83.1 %all-gather.9.cloned.1.call-start = ((), (), s32[]{:S(2)}) async-start(), calls=%async_computation.3 | async-start | bytes 4718592 | tf_op jit(solution)/shard_map/all_gather | solution.py:87
  36.1 80.3 %all-gather.11.cloned.1.call-start = ((), (), s32[]{:S(2)}) async-start(), calls=%async_computation.4 | async-start | bytes 12582912 | tf_op jit(solution)/shard_map/all_gather | solution.py:88
  89.6 1.2 copy-start
  89.6 26.7 %copy-start.1 = (f32[4096]{0:T(1024)S(1)}, f32[4096]{0:T(1024)}, u32[]{:S(2)}) copy-start(f32[4096]{0:T(1024)} %param.9) | copy-start | bytes 49156
  89.6 71.3 %all-gather.13.cloned.1.call-start = ((), (), s32[]{:S(2)}) async-start(), calls=%async_computation.5 | async-start | bytes 2359296 | tf_op jit(solution)/shard_map/all_gather | solution.py:93
  121.7 39.2 %copy-start.2 = (s32[1,32]{1,0:T(1,128)S(1)}, s32[1,32]{1,0:T(1,128)}, u32[]{:S(2)}) copy-start(s32[1,32]{1,0:T(1,128)} %param.15) | copy-start | bytes 388
  121.7 40.0 %copy-start.3 = (s32[1,16]{1,0:T(1,128)S(1)}, s32[1,16]{1,0:T(1,128)}, u32[]{:S(2)}) copy-start(s32[1,16]{1,0:T(1,128)} %param.14) | copy-start | bytes 196
  121.8 65.3 %all-gather.15.cloned.1.call-start = ((), (), s32[]{:S(2)}) async-start(), calls=%async_computation.6 | async-start | bytes 6291456 | tf_op jit(solution)/shard_map/all_gather | solution.py:94
Sparse Core Ops, SparseCore 0:
  36.2 53.3 all-gather.8
  91.4 24.8 all-gather.10
  121.9 38.9 all-gather.12
  162.6 24.4 all-gather.14

commit v6 on v4

--- a/solution.py
+++ b/solution.py
@@ -11,6 +11,7 @@
 KV_HEADS = 4
 HEAD = 128
 DOC_BLOCK = 128
+MOST_BLK = 8
 
 
 def attn_kernel(q_ref, do_ref, k_ref, v_ref, qpos_ref, qdoc_ref, kpos_ref, kdoc_ref,
@@ -31,7 +32,7 @@
         scores = jnp.where(allowed, raw * score_scale, -jnp.inf)
         row_max = jnp.max(scores, axis=1, keepdims=True)
         raised = jnp.exp(scores - row_max)
-        soft = raised / jnp.sum(raised, axis=1, keepdims=True)
+        soft = raised * (1.0 / jnp.sum(raised, axis=1, keepdims=True))
         soft_half = soft.astype(jnp.bfloat16)
         attn = jnp.dot(soft_half, value_block, preferred_element_type=jnp.float32)
         delta = jnp.sum(attn * do_h.astype(jnp.float32), axis=1, keepdims=True)
@@ -46,30 +47,30 @@
     out_ref[:, HEAD:] = vg_acc[...].astype(out_ref.dtype)
 
 
-def attend_all(queries, d_out, all_kv, qpos, qdoc, kpos, kdoc, kv_heads):
+def attend_all(queries, d_out, packed_kv, qpos, qdoc, kpos, kdoc, kv_heads, slot_rows):
     tok_rows, width = queries.shape
-    seq_len = all_kv.shape[0]
+    q_slots, live_len = packed_kv.shape[0], packed_kv.shape[1]
     group_size = width // (kv_heads * HEAD)
     kern = functools.partial(attn_kernel, group_size=group_size, score_scale=HEAD ** (-0.5))
     gw = group_size * HEAD
     return pl.pallas_call(
         kern,
-        grid=(kv_heads,),
+        grid=(kv_heads, q_slots),
         in_specs=[
-            pl.BlockSpec((tok_rows, gw), lambda g: (0, g)),
-            pl.BlockSpec((tok_rows, gw), lambda g: (0, g)),
-            pl.BlockSpec((seq_len, HEAD), lambda g: (0, 2 * g)),
-            pl.BlockSpec((seq_len, HEAD), lambda g: (0, 2 * g + 1)),
-            pl.BlockSpec((tok_rows, 1), lambda g: (0, 0)),
-            pl.BlockSpec((tok_rows, 1), lambda g: (0, 0)),
-            pl.BlockSpec((1, seq_len), lambda g: (0, 0)),
-            pl.BlockSpec((1, seq_len), lambda g: (0, 0)),
+            pl.BlockSpec((slot_rows, gw), lambda g, s: (s, g)),
+            pl.BlockSpec((slot_rows, gw), lambda g, s: (s, g)),
+            pl.BlockSpec((None, live_len, HEAD), lambda g, s: (s, 0, 2 * g)),
+            pl.BlockSpec((None, live_len, HEAD), lambda g, s: (s, 0, 2 * g + 1)),
+            pl.BlockSpec((slot_rows, 1), lambda g, s: (s, 0)),
+            pl.BlockSpec((slot_rows, 1), lambda g, s: (s, 0)),
+            pl.BlockSpec((None, 1, live_len), lambda g, s: (s, 0, 0)),
+            pl.BlockSpec((None, 1, live_len), lambda g, s: (s, 0, 0)),
         ],
-        out_specs=pl.BlockSpec((seq_len, 2 * HEAD), lambda g: (0, g)),
-        out_shape=jax.ShapeDtypeStruct((seq_len, 2 * kv_heads * HEAD), jnp.bfloat16),
-        scratch_shapes=[pltpu.VMEM((seq_len, HEAD), jnp.float32),
-                        pltpu.VMEM((seq_len, HEAD), jnp.float32)],
-    )(queries, d_out, all_kv, all_kv, qpos, qdoc, kpos, kdoc)
+        out_specs=pl.BlockSpec((None, live_len, 2 * HEAD), lambda g, s: (s, 0, g)),
+        out_shape=jax.ShapeDtypeStruct((q_slots, live_len, 2 * kv_heads * HEAD), jnp.float32),
+        scratch_shapes=[pltpu.VMEM((live_len, HEAD), jnp.float32),
+                        pltpu.VMEM((live_len, HEAD), jnp.float32)],
+    )(queries, d_out, packed_kv, packed_kv, qpos, qdoc, kpos, kdoc)
 
 
 CTX = ("chip", "core")
@@ -129,10 +130,32 @@
     row_start = lax.axis_index(CTX) * tok_rows
     query_pos = lax.dynamic_slice_in_dim(key_pos, row_start, tok_rows)
     query_doc = lax.dynamic_slice_in_dim(key_doc, row_start, tok_rows)
-    grad_terms = attend_all(
-        queries[0], d_out[0], all_kv, query_pos[:, None], query_doc[:, None],
-        key_pos[None, :], key_doc[None, :], KV_HEADS,
+    n_slots = seq_len // half_len
+    q_slots = tok_rows // half_len
+    live_slots = min(n_slots, MOST_BLK * DOC_BLOCK // half_len)
+    slot_pos = key_pos.reshape(n_slots, half_len)[:, 0]
+    slot_doc = key_doc.reshape(n_slots, half_len)[:, 0]
+    own_slots = lax.axis_index(CTX) * q_slots + jnp.arange(q_slots, dtype=jnp.int32)
+    live = (slot_doc[None, :] == slot_doc[own_slots][:, None]) & (
+        slot_pos[None, :] <= slot_pos[own_slots][:, None]
     )
+    slot_ids = jnp.arange(n_slots, dtype=jnp.int32)
+    rank = jnp.where(live, 0, n_slots) + slot_ids[None, :]
+    picked = jnp.argsort(rank, axis=1)[:, :live_slots]
+    valid = jnp.take_along_axis(live, picked, axis=1)
+    packed_kv = all_kv.reshape(n_slots, half_len, -1)[picked].reshape(q_slots, live_slots * half_len, -1)
+    far = jnp.int32(seq_len)
+    packed_pos = jnp.where(valid[:, :, None], key_pos.reshape(n_slots, half_len)[picked], far)
+    packed_doc = key_doc.reshape(n_slots, half_len)[picked]
+    packed_terms = attend_all(
+        queries[0], d_out[0], packed_kv, query_pos[:, None], query_doc[:, None],
+        packed_pos.reshape(q_slots, 1, -1), packed_doc.reshape(q_slots, 1, -1), KV_HEADS, half_len,
+    )
+    grad_terms = jnp.zeros((n_slots, half_len, packed_terms.shape[-1]), jnp.float32)
+    grad_terms = grad_terms.at[picked.reshape(-1)].add(
+        packed_terms.reshape(q_slots * live_slots, half_len, -1)
+    )
+    grad_terms = grad_terms.reshape(seq_len, -1).astype(jnp.bfloat16)
     own_sum = scatter_sum(grad_terms, tok_rows)
     contract = (((1,), (1,)), ((), ()))
     grad_normed = lax.dot_general(own_sum, weights, contract, preferred_element_type=jnp.float32)

time: 249 us -> 294 us (1.18)
  other arithmetic: 8.28 us -> 31.5 us
  Pallas kernels: 51 us -> 66.7 us
  local copies, waits for them, and re-layouts: 6.67 us -> 19.4 us
  waiting for transfers between devices: 91.7 us -> 85.6 us
    scatter-add x0 -> x1, other arithmetic: none -> 18.8 us  [body(): grad_terms.at[picked.reshape(-1)]]
    pallas_call x1, Pallas kernels: 51 us -> 66.7 us  [attend_all(): pl.pallas_call(kern, grid=(kv_heads, q_slots), in_specs=[pl.BlockSpec((sl...]
    gather x0 -> x10, local copies, waits for them, and re-layouts: none -> 8.45 us  [the longest x1 4.92 us: body(): all_kv.reshape(n_slots, half_len, -1)[picked]]
    all_gather x1, waiting for transfers between devices: 38.3 us -> 32.2 us  [body(): all_kv = lax.all_gather(local_kv, CTX, axis=0, tiled=True)]
    broadcast_in_dim x0 -> x2, local copies, waits for them, and re-layouts: none -> 4.37 us  [the longest x1 4.29 us: body(): jnp.zeros((n_slots, half_len, packed_terms.shape[-1]), jnp.float32)]
    convert_element_type x0 -> x1, other arithmetic: none -> 4.04 us  [body(): grad_terms = grad_terms.reshape(seq_len, -1).astype(jnp.bfloat16)]
  transfers between devices with their start and end apart: 2 -> 2, of which waited for: 2 -> 2; matrix products, arithmetic and copies ran while one was open for 1% -> 3% of each run, Pallas kernels for 0% -> 0%
where the time goes in v6:
time: 294 us
  waiting for transfers between devices  85.6 us (29%)
  Pallas kernels  66.7 us (23%)
  blocking collectives  65.2 us (22%)
  other arithmetic  31.5 us (11%)
  local copies, waits for them, and re-layouts  19.4 us (7%)
  between operations  13.6 us (5%)
  matrix products  11.8 us (4%)
    pallas_call x1, Pallas kernels, attend_all(): pl.pallas_call(kern, grid=(kv_heads, q_slots), in_specs=[pl.BlockSpec((sl...  66.7 us
    all_gather x1, waiting for transfers between devices, gather_weights(): full = lax.all_gather(by_shard, CTX, axis=1, tiled=False)  53.3 us
    all_gather x1, waiting for transfers between devices, body(): all_kv = lax.all_gather(local_kv, CTX, axis=0, tiled=True)  32.2 us
    all_to_all x1, blocking collectives, scatter_sum(): mine = lax.all_to_all(mine, 'chip', 0, 0, tiled=False)  30.2 us
    all_to_all x1, blocking collectives, gather_weights(): by_shard = lax.all_to_all(spread, 'dp', 0, 0, tiled=False)  26.9 us
    scatter-add x1, other arithmetic, body(): grad_terms.at[picked.reshape(-1)]  18.8 us
    all_to_all x1, blocking collectives, scatter_sum(): lax.all_to_all(terms.reshape(chip_ways, core_ways, tok_rows, width), 'cor...  8.12 us
    dot_general x1, matrix products, body(): lax.dot_general(own_sum, weights, contract, preferred_element_type=jnp.fl...  6.36 us
  transfers between devices with their start and end apart: 2, of which 2 were waited for; matrix products, arithmetic and copies ran while one was open for 3% of the time, Pallas kernels for 0%

profile of v6, /device:TPU:1, one launch (start us, length us, event | category | flops | bytes accessed | tf_op | source)
XLA Modules:
  0.0 293.8 jit_solution(17646326361350164930)
XLA Ops:
  6.5 1.1 copy.47
  7.6 1.1 copy.48
  8.8 0.1 constant_dynamic-slice_fusion
  9.1 26.9 %all_to_all.15 = bf16[16,16,1024]{2,1,0:T(8,128)(2,1)} all-to-all(bf16[16,16,1024]{2,1,0:T(8,128)(2,1)S(1)} %broadcast_in_dim.100), channel_id=1, replica_groups=mesh['dp'=16,'chip'=8,'core'=2] {'dp'}, dimensions={0} | all-to-all | bytes 1048576 | tf_op jit(solution)/shard_map/all_to_all | solution.py:86
  36.2 0.3 fusion.3
  36.5 53.3 %all-gather.6.cloned.1.call-done = bf16[16,256,1024]{2,1,0:T(8,128)(2,1)} async-done(((bf16[16,16,1024]{2,1,0:T(8,128)(2,1)}), bf16[16,256,1024]{2,1,0:T(8,128)(2,1)}) %all-gather.6.cloned.1.call-update) | async-done | bytes 8388624 | tf_op jit(solution)/shard_map/all_gather | solution.py:87
  89.8 5.4 %convolution_convert_fusion = bf16[128,1024]{1,0:T(8,128)(2,1)} fusion(bf16[4096,1024]{1,0:T(8,128)(2,1)} %bitcast.63, bf16[1,128,4096]{2,1,0:T(8,128)(2,1)S(1)} %copy-done, f32[4096]{0:T(1024)S(1)} %copy-done.1, f32[128]{0:T(128)S(1)} %add_rsqrt_fusion), kind=kOutput, calls=%fused_computation.22 | convolution fusion | flops 1075970048 | bytes 9716224 | tf_op jit(solution)/shard_map/dot_general | solution.py:118
  95.2 0.1 select_reduce_fusion
  95.6 0.1 slice_reduce_fusion
  95.8 0.6 gather_fusion.1
  96.4 0.6 gather_fusion
  97.2 0.8 sort.17
  98.2 0.6 gather_fusion.4
  98.8 0.6 gather_fusion.3
  99.5 0.7 gather_fusion.5
  100.7 0.7 reshape.190.kdoc_ref
  101.5 0.7 select_n.111.kpos_ref
  102.2 0.7 copy.55.qdoc_ref
  103.0 0.7 copy.54.qpos_ref
  103.7 32.2 %all-gather.4.cloned.1.call-done = bf16[2048,1024]{1,0:T(8,128)(2,1)} async-done(((bf16[128,1024]{1,0:T(8,128)(2,1)}), bf16[2048,1024]{1,0:T(8,128)(2,1)}) %all-gather.4.cloned.1.call-update) | async-done | bytes 4194320 | tf_op jit(solution)/shard_map/all_gather | solution.py:119
  135.9 4.9 %gather_fusion.2 = bf16[32,64,1024]{2,1,0:T(8,128)(2,1)} fusion(bf16[32,64,1024]{2,1,0:T(8,128)(2,1)} %bitcast.65, s32[1024]{0:T(1024)S(1)} %pad_clamp_fusion), kind=kCustom, calls=%fused_computation.2 | custom fusion | bytes 8388736 | tf_op jit(solution)/shard_map/gather | solution.py:146
  140.9 66.7 %shard_map.82 = f32[2,1024,1024]{2,1,0:T(8,128)} custom-call(bf16[128,4096]{1,0:T(8,128)(2,1)} %bitcast.69, bf16[128,4096]{1,0:T(8,128)(2,1)} %bitcast.70, bf16[2,1024,1024]{2,1,0:T(8,128)(2,1)} %bitcast.59, bf16[2,1024,1024]{2,1,0:T(8,128)(2,1)} %bitcast.60, s32[128,1]{1,0:T(8,128)} %copy.54.qpos_ref, s32[128,1]{1,0:T(8,128)} %copy.55.qdoc_ref, ...), custom_call_target="tpu_custom_call" | custom-call | tf_op jit(solution)/shard_map/pallas_call | solution.py:56
  207.6 4.3 %broadcast_in_dim.91 = f32[32,64,1024]{2,1,0:T(8,128)} broadcast(f32[]{:T(128)} %constant.79.clone.1), dimensions={} | broadcast | bytes 8388612 | tf_op jit(solution)/shard_map/broadcast_in_dim | solution.py:154
  211.9 18.8 %scatter_fusion = f32[32,64,1024]{2,1,0:T(8,128)} fusion(f32[32,64,1024]{2,1,0:T(8,128)} %broadcast_in_dim.91, s32[32]{0:T(128)S(1)} %fusion.31, f32[32,64,1024]{2,1,0:T(8,128)} %bitcast.61), kind=kCustom, calls=%fused_computation.6 | custom fusion | flops 2097152 | bytes 25165952 | tf_op jit(solution)/shard_map/scatter-add | solution.py:155
  230.6 4.0 %convert_element_type.38 = bf16[32,64,1024]{2,1,0:T(8,128)(2,1)S(1)} convert(f32[32,64,1024]{2,1,0:T(8,128)} %scatter_fusion) | non-fusion elementwise | flops 2097152 | bytes 12582912 | tf_op jit(solution)/shard_map/convert_element_type | solution.py:158
  234.7 0.5 copy.56
  235.2 8.1 %all_to_all.16 = bf16[8,2,128,1024]{3,2,0,1:T(8,128)(2,1)} all-to-all(bf16[8,2,128,1024]{3,2,0,1:T(8,128)(2,1)S(1)} %copy.56), channel_id=1, replica_groups=mesh['dp'=16,'chip'=8,'core'=2] {'core'}, dimensions={1} | all-to-all | bytes 8388608 | tf_op jit(solution)/shard_map/all_to_all | solution.py:95
  243.3 3.5 %reduce_sum.63 = bf16[8,128,1024]{2,1,0:T(8,128)(2,1)S(1)} reduce(bf16[8,2,128,1024]{3,2,0,1:T(8,128)(2,1)} %all_to_all.16, bf16[]{:T(256)} %constant.100.clone.1), dimensions={1}, to_apply=%region_5.6 | reduce | flops 1048576 | bytes 6291458 | tf_op jit(solution)/shard_map/reduce_sum | solution.py:98
  246.8 30.2 %all_to_all.17 = bf16[8,128,1024]{2,1,0:T(8,128)(2,1)} all-to-all(bf16[8,128,1024]{2,1,0:T(8,128)(2,1)S(1)} %reduce_sum.63), channel_id=1, replica_groups=mesh['dp'=16,'chip'=8,'core'=2] {'chip'}, dimensions={0} | all-to-all | bytes 4194304 | tf_op jit(solution)/shard_map/all_to_all | solution.py:99
  277.0 2.0 reduce_sum.64
  278.9 6.4 %fusion.10 = (f32[128]{0:T(128)S(1)}, f32[128,4096]{1,0:T(8,128)S(1)}) fusion(bf16[1,128,4096]{2,1,0:T(8,128)(2,1)S(1)} %copy-done, f32[4096]{0:T(1024)S(1)} %copy-done.1, bf16[128,1024]{1,0:T(8,128)(2,1)S(1)} %reduce_sum.64, bf16[4096,1024]{1,0:T(8,128)(2,1)} %bitcast.64), kind=kOutput, calls=%fused_computation.19 | convolution fusion | flops 1075838848 | bytes 11813376 | tf_op jit(solution)/shard_map/dot_general | solution.py:161
  285.3 1.6 fusion.15
  (44 shorter events, 1.7 us)
Async XLA Ops:
  6.5 83.2 %all-gather.6.cloned.1.call-start = ((), (), s32[]{:S(2)}) async-start(), calls=%async_computation.4 | async-start | bytes 8912896 | tf_op jit(solution)/shard_map/all_gather | solution.py:87
  8.7 27.4 %copy-start = (bf16[1,128,4096]{2,1,0:T(8,128)(2,1)S(1)}, bf16[1,128,4096]{2,1,0:T(8,128)(2,1)}, u32[]{:S(2)}) copy-start(bf16[1,128,4096]{2,1,0:T(8,128)(2,1)} %param.8) | copy-start | bytes 3145732
  8.8 81.0 %copy-start.1 = (f32[4096]{0:T(1024)S(1)}, f32[4096]{0:T(1024)}, u32[]{:S(2)}) copy-start(f32[4096]{0:T(1024)} %param.9) | copy-start | bytes 49156
  36.1 99.8 %all-gather.4.cloned.1.call-start = ((), (), s32[]{:S(2)}) async-start(), calls=%async_computation.3 | async-start | bytes 4456448 | tf_op jit(solution)/shard_map/all_gather | solution.py:119
  89.8 5.5 %copy-start.2 = (s32[1,32]{1,0:T(1,128)S(1)}, s32[1,32]{1,0:T(1,128)}, u32[]{:S(2)}) copy-start(s32[1,32]{1,0:T(1,128)} %param.15) | copy-start | bytes 388
  89.8 5.6 %copy-start.3 = (s32[1,16]{1,0:T(1,128)S(1)}, s32[1,16]{1,0:T(1,128)}, u32[]{:S(2)}) copy-start(s32[1,16]{1,0:T(1,128)} %param.14) | copy-start | bytes 196
Sparse Core Ops, SparseCore 0:
  36.2 53.4 all-gather.5
  95.3 40.5 all-gather.3

commit v7 on v4

--- a/solution.py
+++ b/solution.py
@@ -46,18 +46,18 @@
     out_ref[:, HEAD:] = vg_acc[...].astype(out_ref.dtype)
 
 
-def attend_all(queries, d_out, all_kv, qpos, qdoc, kpos, kdoc, kv_heads):
+def attend_all(queries, d_out, all_kv, qpos, qdoc, kpos, kdoc, kv_heads, first_head):
     tok_rows, width = queries.shape
     seq_len = all_kv.shape[0]
-    group_size = width // (kv_heads * HEAD)
+    group_size = HEADS // KV_HEADS
     kern = functools.partial(attn_kernel, group_size=group_size, score_scale=HEAD ** (-0.5))
     gw = group_size * HEAD
     return pl.pallas_call(
         kern,
         grid=(kv_heads,),
         in_specs=[
-            pl.BlockSpec((tok_rows, gw), lambda g: (0, g)),
-            pl.BlockSpec((tok_rows, gw), lambda g: (0, g)),
+            pl.BlockSpec((tok_rows, gw), lambda g: (0, g + first_head)),
+            pl.BlockSpec((tok_rows, gw), lambda g: (0, g + first_head)),
             pl.BlockSpec((seq_len, HEAD), lambda g: (0, 2 * g)),
             pl.BlockSpec((seq_len, HEAD), lambda g: (0, 2 * g + 1)),
             pl.BlockSpec((tok_rows, 1), lambda g: (0, 0)),
@@ -113,9 +113,15 @@
         [w_key.reshape(shard_rows, KV_HEADS, HEAD), w_value.reshape(shard_rows, KV_HEADS, HEAD)],
         axis=2,
     ).reshape(shard_rows, 2 * KV_HEADS * HEAD)
-    weights = gather_weights(local_w, ctx_ways)
-    local_kv = jnp.dot(normed, weights, preferred_element_type=jnp.float32).astype(jnp.bfloat16)
-    all_kv = lax.all_gather(local_kv, CTX, axis=0, tiled=True)
+    halves = 2
+    half_w = local_w.shape[1] // halves
+    weights = []
+    kv_parts = []
+    for part in range(halves):
+        part_w = gather_weights(local_w[:, part * half_w : (part + 1) * half_w], ctx_ways)
+        part_kv = jnp.dot(normed, part_w, preferred_element_type=jnp.float32).astype(jnp.bfloat16)
+        weights.append(part_w)
+        kv_parts.append(lax.all_gather(part_kv, CTX, axis=0, tiled=True))
     row_ids = jnp.arange(seq_len, dtype=jnp.int32)
     slot_hit = (row_ids // half_len)[:, None] == jnp.arange(2 * ctx_ways, dtype=jnp.int32)[None, :]
     key_pos = (
@@ -129,13 +135,24 @@
     row_start = lax.axis_index(CTX) * tok_rows
     query_pos = lax.dynamic_slice_in_dim(key_pos, row_start, tok_rows)
     query_doc = lax.dynamic_slice_in_dim(key_doc, row_start, tok_rows)
-    grad_terms = attend_all(
-        queries[0], d_out[0], all_kv, query_pos[:, None], query_doc[:, None],
-        key_pos[None, :], key_doc[None, :], KV_HEADS,
+    part_heads = KV_HEADS // halves
+    grad_parts = [
+        attend_all(
+            queries[0], d_out[0], kv_parts[part], query_pos[:, None], query_doc[:, None],
+            key_pos[None, :], key_doc[None, :], part_heads, part * part_heads,
+        )
+        for part in range(halves)
+    ]
+    own_sum = scatter_sum(jnp.concatenate(grad_parts, axis=1), tok_rows)
+    contract = (((1,), (1,)), ((), ()))
+    grad_normed = lax.dot_general(
+        own_sum[:, :half_w], weights[0], contract, preferred_element_type=jnp.float32
     )
-    own_sum = scatter_sum(grad_terms, tok_rows)
-    contract = (((1,), (1,)), ((), ()))
-    grad_normed = lax.dot_general(own_sum, weights, contract, preferred_element_type=jnp.float32)
+    for part in range(1, halves):
+        grad_normed = grad_normed + lax.dot_general(
+            own_sum[:, part * half_w : (part + 1) * half_w], weights[part], contract,
+            preferred_element_type=jnp.float32,
+        )
     mean_term = jnp.mean(as_float * norm_gain * grad_normed, axis=-1, keepdims=True)
     grad_embed = (
         inv_rms * norm_gain * grad_normed - as_float * inv_rms * inv_rms * inv_rms * mean_term

time: 249 us -> 275 us (1.10)
  waiting for transfers between devices: 91.7 us -> 105 us
  blocking collectives: 65.2 us -> 75.2 us
    all_to_all x1 -> x2, blocking collectives: 26.9 us -> 36.7 us  [gather_weights(): by_shard = lax.all_to_all(spread, 'dp', 0, 0, tiled=False)]
    all_gather x1 -> x2, waiting for transfers between devices: 53.3 us -> 61.2 us  [gather_weights(): full = lax.all_gather(by_shard, CTX, axis=1, tiled=False)]
    all_gather x1 -> x2, waiting for transfers between devices: 38.3 us -> 43.5 us  [body(): kv_parts.append(lax.all_gather(part_kv, CTX, axis=0, tiled=True))]
    pallas_call x1 -> x2, Pallas kernels: 51 us -> 53.5 us  [attend_all(): pl.pallas_call(kern, grid=(kv_heads,), in_specs=[pl.BlockSpec((tok_rows,...]
    dot_general x2 -> x4, matrix products: 11.8 us -> 12.6 us  [the longest x2 7.25 us: body(): jnp.dot(normed, part_w, preferred_element_type=jnp.float32)]
  transfers between devices with their start and end apart: 2 -> 4, of which waited for: 2 -> 4; matrix products, arithmetic and copies ran while one was open for 1% -> 4% of each run, Pallas kernels for 0% -> 10%
where the time goes in v7:
time: 275 us
  waiting for transfers between devices  105 us (38%)
  blocking collectives  75.2 us (27%)
  Pallas kernels  53.5 us (19%)
  between operations  13.3 us (5%)
  matrix products  12.6 us (5%)
  other arithmetic  10.4 us (4%)
  local copies, waits for them, and re-layouts  4.61 us (2%)
    all_gather x2, waiting for transfers between devices, gather_weights(): full = lax.all_gather(by_shard, CTX, axis=1, tiled=False)  61.2 us
    pallas_call x2, Pallas kernels, attend_all(): pl.pallas_call(kern, grid=(kv_heads,), in_specs=[pl.BlockSpec((tok_rows,...  53.5 us
    all_gather x2, waiting for transfers between devices, body(): kv_parts.append(lax.all_gather(part_kv, CTX, axis=0, tiled=True))  43.5 us
    all_to_all x2, blocking collectives, gather_weights(): by_shard = lax.all_to_all(spread, 'dp', 0, 0, tiled=False)  36.7 us
    all_to_all x1, blocking collectives, scatter_sum(): mine = lax.all_to_all(mine, 'chip', 0, 0, tiled=False)  30.5 us
    all_to_all x1, blocking collectives, scatter_sum(): lax.all_to_all(terms.reshape(chip_ways, core_ways, tok_rows, width), 'cor...  8.09 us
    dot_general x2, matrix products, body(): jnp.dot(normed, part_w, preferred_element_type=jnp.float32)  7.25 us
  transfers between devices with their start and end apart: 4, of which 4 were waited for; matrix products, arithmetic and copies ran while one was open for 4% of the time, Pallas kernels for 10%

profile of v7, /device:TPU:1, one launch (start us, length us, event | category | flops | bytes accessed | tf_op | source)
XLA Modules:
  0.0 274.6 jit_solution(771726943561130667)
XLA Ops:
  6.5 1.1 copy.30
  7.6 1.1 copy.31
  8.7 0.1 pad_maximum_fusion.1
  8.8 0.1 constant_dynamic-slice_fusion
  9.0 0.1 copy.32
  9.1 21.9 %all_to_all.20 = bf16[16,16,512]{2,1,0:T(8,128)(2,1)} all-to-all(bf16[16,16,512]{2,1,0:T(8,128)(2,1)S(1)} %broadcast_in_dim.40), channel_id=1, replica_groups=mesh['dp'=16,'chip'=8,'core'=2] {'dp'}, dimensions={0} | all-to-all | bytes 524288 | tf_op jit(solution)/shard_map/all_to_all | solution.py:85
  31.1 0.1 copy.35
  31.2 14.7 %all_to_all.21 = bf16[16,16,512]{2,1,0:T(8,128)(2,1)} all-to-all(bf16[16,16,512]{2,1,0:T(8,128)(2,1)S(1)} %broadcast_in_dim.76), channel_id=1, replica_groups=mesh['dp'=16,'chip'=8,'core'=2] {'dp'}, dimensions={0} | all-to-all | bytes 524288 | tf_op jit(solution)/shard_map/all_to_all | solution.py:85
  46.1 0.3 fusion.3
  46.4 24.1 %all-gather.11.cloned.1.call-done = bf16[16,256,512]{2,1,0:T(8,128)(2,1)} async-done(((bf16[16,16,512]{2,1,0:T(8,128)(2,1)}), bf16[16,256,512]{2,1,0:T(8,128)(2,1)}) %all-gather.11.cloned.1.call-update) | async-done | bytes 4194320 | tf_op jit(solution)/shard_map/all_gather | solution.py:86
  70.5 3.6 %convolution_convert_fusion.1 = bf16[128,512]{1,0:T(8,128)(2,1)} fusion(bf16[4096,512]{1,0:T(8,128)(2,1)} %bitcast.55, bf16[1,128,4096]{2,1,0:T(8,128)(2,1)S(1)} %copy-done, f32[4096]{0:T(1024)S(1)} %copy-done.4, f32[128]{0:T(128)S(1)} %add_rsqrt_fusion), kind=kOutput, calls=%fused_computation.18 | convolution fusion | flops 539033600 | bytes 5390848 | tf_op jit(solution)/shard_map/dot_general | solution.py:122
  74.2 37.1 %all-gather.13.cloned.1.call-done = bf16[16,256,512]{2,1,0:T(8,128)(2,1)} async-done(((bf16[16,16,512]{2,1,0:T(8,128)(2,1)}), bf16[16,256,512]{2,1,0:T(8,128)(2,1)}) %all-gather.13.cloned.1.call-update) | async-done | bytes 4194320 | tf_op jit(solution)/shard_map/all_gather | solution.py:86
  111.2 3.6 %convolution_convert_fusion = bf16[128,512]{1,0:T(8,128)(2,1)} fusion(bf16[4096,512]{1,0:T(8,128)(2,1)} %bitcast.53, bf16[1,128,4096]{2,1,0:T(8,128)(2,1)S(1)} %copy-done, f32[4096]{0:T(1024)S(1)} %copy-done.4, f32[128]{0:T(128)S(1)} %add_rsqrt_fusion), kind=kOutput, calls=%fused_computation.17 | convolution fusion | flops 539033600 | bytes 5390848 | tf_op jit(solution)/shard_map/dot_general | solution.py:122
  114.9 0.1 select_reduce_fusion
  115.1 0.1 select_reduce_fusion.1
  115.2 0.1 dynamic-slice_bitcast_fusion
  115.3 0.7 copy.34.qdoc_ref
  116.0 0.7 copy.33.qpos_ref
  116.8 0.6 fusion.26.kpos_ref
  117.4 32.1 %all-gather.7.cloned.1.call-done.k_ref.v_ref = bf16[2048,512]{1,0:T(8,128)(2,1)} async-done(((bf16[128,512]{1,0:T(8,128)(2,1)}), bf16[2048,512]{1,0:T(8,128)(2,1)}) %all-gather.7.cloned.1.call-update) | async-done | bytes 2097168 | tf_op jit(solution)/shard_map/all_gather | solution.py:124
  149.5 26.7 %shard_map.82 = bf16[2048,512]{1,0:T(8,128)(2,1)} custom-call(bf16[128,4096]{1,0:T(8,128)(2,1)} %bitcast.57, bf16[128,4096]{1,0:T(8,128)(2,1)} %bitcast.59, bf16[2048,512]{1,0:T(8,128)(2,1)} %all-gather.7.cloned.1.call-done.k_ref.v_ref, bf16[2048,512]{1,0:T(8,128)(2,1)} %all-gather.7.cloned.1.call-done.k_ref.v_ref, s32[128,1]{1,0:T(8,128)} %copy.33.qpos_ref, ...), custom_call_target="tpu_custom_call" | custom-call | tf_op jit(solution)/shard_map/pallas_call | solution.py:55
  176.2 11.4 %all-gather.9.cloned.1.call-done.k_ref.v_ref = bf16[2048,512]{1,0:T(8,128)(2,1)} async-done(((bf16[128,512]{1,0:T(8,128)(2,1)}), bf16[2048,512]{1,0:T(8,128)(2,1)}) %all-gather.9.cloned.1.call-update) | async-done | bytes 2097168 | tf_op jit(solution)/shard_map/all_gather | solution.py:124
  187.6 26.7 %shard_map.83 = bf16[2048,512]{1,0:T(8,128)(2,1)} custom-call(bf16[128,4096]{1,0:T(8,128)(2,1)} %bitcast.58, bf16[128,4096]{1,0:T(8,128)(2,1)} %bitcast.60, bf16[2048,512]{1,0:T(8,128)(2,1)} %all-gather.9.cloned.1.call-done.k_ref.v_ref, bf16[2048,512]{1,0:T(8,128)(2,1)} %all-gather.9.cloned.1.call-done.k_ref.v_ref, s32[128,1]{1,0:T(8,128)} %copy.33.qpos_ref, ...), custom_call_target="tpu_custom_call" | custom-call | tf_op jit(solution)/shard_map/pallas_call | solution.py:55
  214.4 2.2 pad_maximum_fusion
  216.5 0.4 copy.38
  217.0 8.1 %all_to_all.22 = bf16[8,2,128,1024]{3,2,0,1:T(8,128)(2,1)} all-to-all(bf16[8,2,128,1024]{3,2,0,1:T(8,128)(2,1)S(1)} %copy.38), channel_id=1, replica_groups=mesh['dp'=16,'chip'=8,'core'=2] {'core'}, dimensions={1} | all-to-all | bytes 8388608 | tf_op jit(solution)/shard_map/all_to_all | solution.py:94
  225.1 3.5 %reduce_sum.63 = bf16[8,128,1024]{2,1,0:T(8,128)(2,1)S(1)} reduce(bf16[8,2,128,1024]{3,2,0,1:T(8,128)(2,1)} %all_to_all.22, bf16[]{:T(256)} %constant.77.clone.1), dimensions={1}, to_apply=%region_3.4 | reduce | flops 1048576 | bytes 6291458 | tf_op jit(solution)/shard_map/reduce_sum | solution.py:97
  228.6 30.5 %all_to_all.23 = bf16[8,128,1024]{2,1,0:T(8,128)(2,1)} all-to-all(bf16[8,128,1024]{2,1,0:T(8,128)(2,1)S(1)} %reduce_sum.63), channel_id=1, replica_groups=mesh['dp'=16,'chip'=8,'core'=2] {'chip'}, dimensions={0} | all-to-all | bytes 4194304 | tf_op jit(solution)/shard_map/all_to_all | solution.py:98
  259.0 2.0 reduce_sum.64
  261.0 3.8 %fusion.18 = f32[128,4096]{1,0:T(8,128)S(1)} fusion(bf16[4096,512]{1,0:T(8,128)(2,1)} %bitcast.56, bf16[128,1024]{1,0:T(8,128)(2,1)S(1)} %reduce_sum.64), kind=kOutput, calls=%fused_computation.25 | convolution fusion | flops 536870912 | bytes 6422528 | tf_op jit(solution)/shard_map/dot_general | solution.py:148
  264.8 1.6 fusion.10
  266.4 1.6 fusion.14
  (29 shorter events, 0.4 us)
Async XLA Ops:
  6.5 63.9 %all-gather.11.cloned.1.call-start = ((), (), s32[]{:S(2)}) async-start(), calls=%async_computation.6 | async-start | bytes 4456448 | tf_op jit(solution)/shard_map/all_gather | solution.py:86
  8.8 37.3 %copy-start = (bf16[1,128,4096]{2,1,0:T(8,128)(2,1)S(1)}, bf16[1,128,4096]{2,1,0:T(8,128)(2,1)}, u32[]{:S(2)}) copy-start(bf16[1,128,4096]{2,1,0:T(8,128)(2,1)} %param.8) | copy-start | bytes 3145732
  8.8 61.7 %copy-start.4 = (f32[4096]{0:T(1024)S(1)}, f32[4096]{0:T(1024)}, u32[]{:S(2)}) copy-start(f32[4096]{0:T(1024)} %param.9) | copy-start | bytes 49156
  31.1 80.2 %all-gather.13.cloned.1.call-start = ((), (), s32[]{:S(2)}) async-start(), calls=%async_computation.7 | async-start | bytes 4456448 | tf_op jit(solution)/shard_map/all_gather | solution.py:86
  46.0 103.5 %all-gather.7.cloned.1.call-start = ((), (), s32[]{:S(2)}) async-start(), calls=%async_computation.4 | async-start | bytes 2228224 | tf_op jit(solution)/shard_map/all_gather | solution.py:124
  74.1 113.5 %all-gather.9.cloned.1.call-start = ((), (), s32[]{:S(2)}) async-start(), calls=%async_computation.5 | async-start | bytes 2228224 | tf_op jit(solution)/shard_map/all_gather | solution.py:124
  111.2 3.7 %copy-start.5 = (s32[1,32]{1,0:T(1,128)S(1)}, s32[1,32]{1,0:T(1,128)}, u32[]{:S(2)}) copy-start(s32[1,32]{1,0:T(1,128)} %param.15) | copy-start | bytes 388
  111.2 3.8 %copy-start.6 = (s32[1,16]{1,0:T(1,128)S(1)}, s32[1,16]{1,0:T(1,128)}, u32[]{:S(2)}) copy-start(s32[1,16]{1,0:T(1,128)} %param.14) | copy-start | bytes 196
  115.2 34.3 %copy-start.3 = (s32[2048]{0:T(1024)}, s32[2048]{0:T(1024)S(1)}, u32[]{:S(2)}) copy-start(s32[2048]{0:T(1024)S(1)} %select_reduce_fusion.1) | copy-start | bytes 24580
  176.2 38.1 %copy-start.1 = (bf16[2048,512]{1,0:T(8,128)(2,1)S(1)}, bf16[2048,512]{1,0:T(8,128)(2,1)}, u32[]{:S(2)}) copy-start(bf16[2048,512]{1,0:T(8,128)(2,1)} %shard_map.82) | copy-start | bytes 6291460
  261.0 3.8 %copy-start.2 = (bf16[16,256,512]{2,1,0:T(8,128)(2,1)S(1)}, bf16[16,256,512]{2,1,0:T(8,128)(2,1)}, u32[]{:S(2)}) copy-start(bf16[16,256,512]{2,1,0:T(8,128)(2,1)} %all-gather.13.cloned.1.call-done) | copy-start | bytes 12582916
Sparse Core Ops, SparseCore 0:
  31.2 39.2 all-gather.10
  72.3 38.9 all-gather.12
  113.1 36.3 all-gather.6
  151.2 36.3 all-gather.8

commit v8 on v4

--- a/solution.py
+++ b/solution.py
@@ -31,7 +31,7 @@
         scores = jnp.where(allowed, raw * score_scale, -jnp.inf)
         row_max = jnp.max(scores, axis=1, keepdims=True)
         raised = jnp.exp(scores - row_max)
-        soft = raised / jnp.sum(raised, axis=1, keepdims=True)
+        soft = raised * (1.0 / jnp.sum(raised, axis=1, keepdims=True))
         soft_half = soft.astype(jnp.bfloat16)
         attn = jnp.dot(soft_half, value_block, preferred_element_type=jnp.float32)
         delta = jnp.sum(attn * do_h.astype(jnp.float32), axis=1, keepdims=True)

time: 249 us -> 249 us (level)
  no operation moved by 1% of the time
where the time goes in v8:
time: 249 us; the launch traced here: 248 us
  waiting for transfers between devices  91.7 us (37%)
  blocking collectives  65.2 us (26%)
  Pallas kernels  51 us (20%)
  between operations  13.5 us (5%)
  matrix products  11.8 us (5%)
  other arithmetic  8.28 us (3%)
  local copies, waits for them, and re-layouts  6.67 us (3%)
    all_gather x1, waiting for transfers between devices, gather_weights(): full = lax.all_gather(by_shard, CTX, axis=1, tiled=False)  53.3 us
    pallas_call x1, Pallas kernels, attend_all(): pl.pallas_call(kern, grid=(kv_heads,), in_specs=[pl.BlockSpec((tok_rows,...  51 us
    all_gather x1, waiting for transfers between devices, body(): all_kv = lax.all_gather(local_kv, CTX, axis=0, tiled=True)  38.3 us
    all_to_all x1, blocking collectives, scatter_sum(): mine = lax.all_to_all(mine, 'chip', 0, 0, tiled=False)  30.1 us
    all_to_all x1, blocking collectives, gather_weights(): by_shard = lax.all_to_all(spread, 'dp', 0, 0, tiled=False)  26.9 us
    all_to_all x1, blocking collectives, scatter_sum(): lax.all_to_all(terms.reshape(chip_ways, core_ways, tok_rows, width), 'cor...  8.15 us
    dot_general x1, matrix products, body(): lax.dot_general(own_sum, weights, contract, preferred_element_type=jnp.fl...  6.36 us
    dot_general x1, matrix products, body(): jnp.dot(normed, weights, preferred_element_type=jnp.float32)  5.41 us
  transfers between devices with their start and end apart: 2, of which 2 were waited for; matrix products, arithmetic and copies ran while one was open for 1% of the time, Pallas kernels for 0%

profile of v8, /device:TPU:1, one launch (start us, length us, event | category | flops | bytes accessed | tf_op | source)
XLA Modules:
  0.0 248.2 jit_solution(16189277756060579677)
XLA Ops:
  6.5 1.1 copy.22
  7.6 1.1 copy.23
  8.7 0.0 copy-start
  8.7 0.1 pad_maximum_fusion
  8.8 0.0 copy-start.1
  8.8 0.1 constant_dynamic-slice_fusion
  9.0 0.1 copy.24
  9.1 0.1 broadcast_in_dim.56
  9.1 26.9 %all_to_all.15 = bf16[16,16,1024]{2,1,0:T(8,128)(2,1)} all-to-all(bf16[16,16,1024]{2,1,0:T(8,128)(2,1)S(1)} %broadcast_in_dim.56), channel_id=1, replica_groups=mesh['dp'=16,'chip'=8,'core'=2] {'dp'}, dimensions={0} | all-to-all | bytes 1048576 | tf_op jit(solution)/shard_map/all_to_all | solution.py:85
  36.1 0.0 all-gather.6.cloned.1.call-update
  36.1 0.0 all-gather.4.cloned.1.call-start
  36.2 0.3 fusion.3
  36.5 53.3 %all-gather.6.cloned.1.call-done = bf16[16,256,1024]{2,1,0:T(8,128)(2,1)} async-done(((bf16[16,16,1024]{2,1,0:T(8,128)(2,1)}), bf16[16,256,1024]{2,1,0:T(8,128)(2,1)}) %all-gather.6.cloned.1.call-update) | async-done | bytes 8388624 | tf_op jit(solution)/shard_map/all_gather | solution.py:86
  89.8 5.4 %convolution_convert_fusion = bf16[128,1024]{1,0:T(8,128)(2,1)} fusion(bf16[4096,1024]{1,0:T(8,128)(2,1)} %bitcast.50, bf16[1,128,4096]{2,1,0:T(8,128)(2,1)S(1)} %copy-done, f32[4096]{0:T(1024)S(1)} %copy-done.1, f32[128]{0:T(128)S(1)} %add_rsqrt_fusion), kind=kOutput, calls=%fused_computation.15 | convolution fusion | flops 1075970048 | bytes 9716224 | tf_op jit(solution)/shard_map/dot_general | solution.py:117
  95.2 0.0 all-gather.4.cloned.1.call-update
  95.2 0.0 copy-done.3
  95.2 0.1 select_reduce_fusion
  95.4 0.1 select_reduce_fusion.1
  95.5 0.1 dynamic-slice_bitcast_fusion
  95.6 0.7 copy.26.qdoc_ref
  96.3 0.7 copy.25.qpos_ref
  97.0 0.6 fusion.24.kpos_ref
  97.6 38.3 %all-gather.4.cloned.1.call-done.k_ref.v_ref = bf16[2048,1024]{1,0:T(8,128)(2,1)} async-done(((bf16[128,1024]{1,0:T(8,128)(2,1)}), bf16[2048,1024]{1,0:T(8,128)(2,1)}) %all-gather.4.cloned.1.call-update) | async-done | bytes 4194320 | tf_op jit(solution)/shard_map/all_gather | solution.py:118
  135.9 0.0 copy-done.2
  135.9 51.0 %shard_map.82 = bf16[2048,1024]{1,0:T(8,128)(2,1)} custom-call(bf16[128,4096]{1,0:T(8,128)(2,1)} %bitcast.53, bf16[128,4096]{1,0:T(8,128)(2,1)} %bitcast.54, bf16[2048,1024]{1,0:T(8,128)(2,1)} %all-gather.4.cloned.1.call-done.k_ref.v_ref, bf16[2048,1024]{1,0:T(8,128)(2,1)} %all-gather.4.cloned.1.call-done.k_ref.v_ref, s32[128,1]{1,0:T(8,128)} %copy.25.qpos_ref, ...), custom_call_target="tpu_custom_call" | custom-call | tf_op jit(solution)/shard_map/pallas_call | solution.py:55
  187.0 2.6 %copy.27 = bf16[8,2,128,1024]{3,2,0,1:T(8,128)(2,1)S(1)} copy(bf16[8,2,128,1024]{3,2,1,0:T(8,128)(2,1)} %bitcast.49) | data formatting | bytes 8388608 | tf_op jit(solution)/shard_map/reshape | solution.py:95
  189.6 8.2 %all_to_all.16 = bf16[8,2,128,1024]{3,2,0,1:T(8,128)(2,1)} all-to-all(bf16[8,2,128,1024]{3,2,0,1:T(8,128)(2,1)S(1)} %copy.27), channel_id=1, replica_groups=mesh['dp'=16,'chip'=8,'core'=2] {'core'}, dimensions={1} | all-to-all | bytes 8388608 | tf_op jit(solution)/shard_map/all_to_all | solution.py:94
  197.8 3.5 %reduce_sum.63 = bf16[8,128,1024]{2,1,0:T(8,128)(2,1)S(1)} reduce(bf16[8,2,128,1024]{3,2,0,1:T(8,128)(2,1)} %all_to_all.16, bf16[]{:T(256)} %constant.77.clone.1), dimensions={1}, to_apply=%region_3.4 | reduce | flops 1048576 | bytes 6291458 | tf_op jit(solution)/shard_map/reduce_sum | solution.py:97
  201.3 30.1 %all_to_all.17 = bf16[8,128,1024]{2,1,0:T(8,128)(2,1)} all-to-all(bf16[8,128,1024]{2,1,0:T(8,128)(2,1)S(1)} %reduce_sum.63), channel_id=1, replica_groups=mesh['dp'=16,'chip'=8,'core'=2] {'chip'}, dimensions={0} | all-to-all | bytes 4194304 | tf_op jit(solution)/shard_map/all_to_all | solution.py:98
  231.4 2.0 reduce_sum.64
  233.3 6.4 %fusion.10 = (f32[128]{0:T(128)S(1)}, f32[128,4096]{1,0:T(8,128)S(1)}) fusion(bf16[1,128,4096]{2,1,0:T(8,128)(2,1)S(1)} %copy-done, f32[4096]{0:T(1024)S(1)} %copy-done.1, bf16[128,1024]{1,0:T(8,128)(2,1)S(1)} %reduce_sum.64, bf16[4096,1024]{1,0:T(8,128)(2,1)} %bitcast.51), kind=kOutput, calls=%fused_computation.12 | convolution fusion | flops 1075838848 | bytes 11813376 | tf_op jit(solution)/shard_map/dot_general | solution.py:138
  239.7 1.6 fusion.15
  (11 shorter events, 0.0 us)
Async XLA Ops:
  6.5 83.2 %all-gather.6.cloned.1.call-start = ((), (), s32[]{:S(2)}) async-start(), calls=%async_computation.4 | async-start | bytes 8912896 | tf_op jit(solution)/shard_map/all_gather | solution.py:86
  8.7 27.4 %copy-start = (bf16[1,128,4096]{2,1,0:T(8,128)(2,1)S(1)}, bf16[1,128,4096]{2,1,0:T(8,128)(2,1)}, u32[]{:S(2)}) copy-start(bf16[1,128,4096]{2,1,0:T(8,128)(2,1)} %param.8) | copy-start | bytes 3145732
  8.8 81.0 %copy-start.1 = (f32[4096]{0:T(1024)S(1)}, f32[4096]{0:T(1024)}, u32[]{:S(2)}) copy-start(f32[4096]{0:T(1024)} %param.9) | copy-start | bytes 49156
  36.1 99.8 %all-gather.4.cloned.1.call-start = ((), (), s32[]{:S(2)}) async-start(), calls=%async_computation.3 | async-start | bytes 4456448 | tf_op jit(solution)/shard_map/all_gather | solution.py:118
  89.8 5.5 %copy-start.3 = (s32[1,32]{1,0:T(1,128)S(1)}, s32[1,32]{1,0:T(1,128)}, u32[]{:S(2)}) copy-start(s32[1,32]{1,0:T(1,128)} %param.15) | copy-start | bytes 388
  89.8 5.6 %copy-start.4 = (s32[1,16]{1,0:T(1,128)S(1)}, s32[1,16]{1,0:T(1,128)}, u32[]{:S(2)}) copy-start(s32[1,16]{1,0:T(1,128)} %param.14) | copy-start | bytes 196
  95.5 40.5 %copy-start.2 = (s32[2048]{0:T(1024)}, s32[2048]{0:T(1024)S(1)}, u32[]{:S(2)}) copy-start(s32[2048]{0:T(1024)S(1)} %select_reduce_fusion.1) | copy-start | bytes 24580
Sparse Core Ops, SparseCore 0:
  36.2 53.4 all-gather.5
  95.3 40.5 all-gather.3

commit v9 on v8

--- a/solution.py
+++ b/solution.py
@@ -41,7 +41,7 @@
         vg_acc[...] += lax.dot_general(soft_half, do_h, tn, preferred_element_type=jnp.float32)
         return carry
 
-    lax.fori_loop(0, group_size, head_step, 0)
+    lax.fori_loop(0, group_size, head_step, 0, unroll=True)
     out_ref[:, :HEAD] = kg_acc[...].astype(out_ref.dtype)
     out_ref[:, HEAD:] = vg_acc[...].astype(out_ref.dtype)
 

time: 249 us -> 243 us (0.976)
  Pallas kernels: 51 us -> 45 us
    pallas_call x1, Pallas kernels: 51 us -> 45 us  [attend_all(): pl.pallas_call(kern, grid=(kv_heads,), in_specs=[pl.BlockSpec((tok_rows,...]
where the time goes in v9:
time: 243 us
  waiting for transfers between devices  91.6 us (38%)
  blocking collectives  65.7 us (27%)
  Pallas kernels  45 us (19%)
  between operations  13.5 us (6%)
  matrix products  11.8 us (5%)
  other arithmetic  8.28 us (3%)
  local copies, waits for them, and re-layouts  6.67 us (3%)
    all_gather x1, waiting for transfers between devices, gather_weights(): full = lax.all_gather(by_shard, CTX, axis=1, tiled=False)  53.3 us
    pallas_call x1, Pallas kernels, attend_all(): pl.pallas_call(kern, grid=(kv_heads,), in_specs=[pl.BlockSpec((tok_rows,...  45 us
    all_gather x1, waiting for transfers between devices, body(): all_kv = lax.all_gather(local_kv, CTX, axis=0, tiled=True)  38.3 us
    all_to_all x1, blocking collectives, scatter_sum(): mine = lax.all_to_all(mine, 'chip', 0, 0, tiled=False)  30.5 us
    all_to_all x1, blocking collectives, gather_weights(): by_shard = lax.all_to_all(spread, 'dp', 0, 0, tiled=False)  26.9 us
    all_to_all x1, blocking collectives, scatter_sum(): lax.all_to_all(terms.reshape(chip_ways, core_ways, tok_rows, width), 'cor...  8.19 us
    dot_general x1, matrix products, body(): lax.dot_general(own_sum, weights, contract, preferred_element_type=jnp.fl...  6.36 us
    dot_general x1, matrix products, body(): jnp.dot(normed, weights, preferred_element_type=jnp.float32)  5.42 us
  transfers between devices with their start and end apart: 2, of which 2 were waited for; matrix products, arithmetic and copies ran while one was open for 1% of the time, Pallas kernels for 0%

profile of v9, /device:TPU:1, one launch (start us, length us, event | category | flops | bytes accessed | tf_op | source)
XLA Modules:
  0.0 242.6 jit_solution(17003493325715444022)
XLA Ops:
  6.5 1.1 copy.22
  7.6 1.1 copy.23
  8.7 0.0 copy-start
  8.7 0.1 pad_maximum_fusion
  8.8 0.0 copy-start.1
  8.8 0.1 constant_dynamic-slice_fusion
  9.0 0.1 copy.24
  9.1 0.1 broadcast_in_dim.56
  9.1 26.9 %all_to_all.15 = bf16[16,16,1024]{2,1,0:T(8,128)(2,1)} all-to-all(bf16[16,16,1024]{2,1,0:T(8,128)(2,1)S(1)} %broadcast_in_dim.56), channel_id=1, replica_groups=mesh['dp'=16,'chip'=8,'core'=2] {'dp'}, dimensions={0} | all-to-all | bytes 1048576 | tf_op jit(solution)/shard_map/all_to_all | solution.py:85
  36.1 0.0 all-gather.6.cloned.1.call-update
  36.1 0.0 all-gather.4.cloned.1.call-start
  36.2 0.3 fusion.3
  36.5 53.3 %all-gather.6.cloned.1.call-done = bf16[16,256,1024]{2,1,0:T(8,128)(2,1)} async-done(((bf16[16,16,1024]{2,1,0:T(8,128)(2,1)}), bf16[16,256,1024]{2,1,0:T(8,128)(2,1)}) %all-gather.6.cloned.1.call-update) | async-done | bytes 8388624 | tf_op jit(solution)/shard_map/all_gather | solution.py:86
  89.8 0.0 copy-done.1
  89.8 5.4 %convolution_convert_fusion = bf16[128,1024]{1,0:T(8,128)(2,1)} fusion(bf16[4096,1024]{1,0:T(8,128)(2,1)} %bitcast.50, bf16[1,128,4096]{2,1,0:T(8,128)(2,1)S(1)} %copy-done, f32[4096]{0:T(1024)S(1)} %copy-done.1, f32[128]{0:T(128)S(1)} %add_rsqrt_fusion), kind=kOutput, calls=%fused_computation.15 | convolution fusion | flops 1075970048 | bytes 9716224 | tf_op jit(solution)/shard_map/dot_general | solution.py:117
  95.2 0.0 all-gather.4.cloned.1.call-update
  95.2 0.0 copy-done.3
  95.2 0.1 select_reduce_fusion
  95.4 0.1 select_reduce_fusion.1
  95.5 0.1 dynamic-slice_bitcast_fusion
  95.6 0.7 copy.26.qdoc_ref
  96.3 0.7 copy.25.qpos_ref
  97.0 0.6 fusion.24.kpos_ref
  97.6 38.3 %all-gather.4.cloned.1.call-done.k_ref.v_ref = bf16[2048,1024]{1,0:T(8,128)(2,1)} async-done(((bf16[128,1024]{1,0:T(8,128)(2,1)}), bf16[2048,1024]{1,0:T(8,128)(2,1)}) %all-gather.4.cloned.1.call-update) | async-done | bytes 4194320 | tf_op jit(solution)/shard_map/all_gather | solution.py:118
  135.9 45.0 %shard_map.82 = bf16[2048,1024]{1,0:T(8,128)(2,1)} custom-call(bf16[128,4096]{1,0:T(8,128)(2,1)} %bitcast.53, bf16[128,4096]{1,0:T(8,128)(2,1)} %bitcast.54, bf16[2048,1024]{1,0:T(8,128)(2,1)} %all-gather.4.cloned.1.call-done.k_ref.v_ref, bf16[2048,1024]{1,0:T(8,128)(2,1)} %all-gather.4.cloned.1.call-done.k_ref.v_ref, s32[128,1]{1,0:T(8,128)} %copy.25.qpos_ref, ...), custom_call_target="tpu_custom_call" | custom-call | tf_op jit(solution)/shard_map/pallas_call | solution.py:55
  180.9 2.6 %copy.27 = bf16[8,2,128,1024]{3,2,0,1:T(8,128)(2,1)S(1)} copy(bf16[8,2,128,1024]{3,2,1,0:T(8,128)(2,1)} %bitcast.49) | data formatting | bytes 8388608 | tf_op jit(solution)/shard_map/reshape | solution.py:95
  183.5 8.2 %all_to_all.16 = bf16[8,2,128,1024]{3,2,0,1:T(8,128)(2,1)} all-to-all(bf16[8,2,128,1024]{3,2,0,1:T(8,128)(2,1)S(1)} %copy.27), channel_id=1, replica_groups=mesh['dp'=16,'chip'=8,'core'=2] {'core'}, dimensions={1} | all-to-all | bytes 8388608 | tf_op jit(solution)/shard_map/all_to_all | solution.py:94
  191.7 3.5 %reduce_sum.63 = bf16[8,128,1024]{2,1,0:T(8,128)(2,1)S(1)} reduce(bf16[8,2,128,1024]{3,2,0,1:T(8,128)(2,1)} %all_to_all.16, bf16[]{:T(256)} %constant.77.clone.1), dimensions={1}, to_apply=%region_3.4 | reduce | flops 1048576 | bytes 6291458 | tf_op jit(solution)/shard_map/reduce_sum | solution.py:97
  195.2 30.5 %all_to_all.17 = bf16[8,128,1024]{2,1,0:T(8,128)(2,1)} all-to-all(bf16[8,128,1024]{2,1,0:T(8,128)(2,1)S(1)} %reduce_sum.63), channel_id=1, replica_groups=mesh['dp'=16,'chip'=8,'core'=2] {'chip'}, dimensions={0} | all-to-all | bytes 4194304 | tf_op jit(solution)/shard_map/all_to_all | solution.py:98
  225.8 2.0 reduce_sum.64
  227.7 6.4 %fusion.10 = (f32[128]{0:T(128)S(1)}, f32[128,4096]{1,0:T(8,128)S(1)}) fusion(bf16[1,128,4096]{2,1,0:T(8,128)(2,1)S(1)} %copy-done, f32[4096]{0:T(1024)S(1)} %copy-done.1, bf16[128,1024]{1,0:T(8,128)(2,1)S(1)} %reduce_sum.64, bf16[4096,1024]{1,0:T(8,128)(2,1)} %bitcast.51), kind=kOutput, calls=%fused_computation.12 | convolution fusion | flops 1075838848 | bytes 11813376 | tf_op jit(solution)/shard_map/dot_general | solution.py:138
  234.1 1.6 fusion.15
  (11 shorter events, 0.0 us)
Async XLA Ops:
  6.5 83.2 %all-gather.6.cloned.1.call-start = ((), (), s32[]{:S(2)}) async-start(), calls=%async_computation.4 | async-start | bytes 8912896 | tf_op jit(solution)/shard_map/all_gather | solution.py:86
  8.7 27.4 %copy-start = (bf16[1,128,4096]{2,1,0:T(8,128)(2,1)S(1)}, bf16[1,128,4096]{2,1,0:T(8,128)(2,1)}, u32[]{:S(2)}) copy-start(bf16[1,128,4096]{2,1,0:T(8,128)(2,1)} %param.8) | copy-start | bytes 3145732
  8.8 81.0 %copy-start.1 = (f32[4096]{0:T(1024)S(1)}, f32[4096]{0:T(1024)}, u32[]{:S(2)}) copy-start(f32[4096]{0:T(1024)} %param.9) | copy-start | bytes 49156
  36.1 99.8 %all-gather.4.cloned.1.call-start = ((), (), s32[]{:S(2)}) async-start(), calls=%async_computation.3 | async-start | bytes 4456448 | tf_op jit(solution)/shard_map/all_gather | solution.py:118
  89.8 5.5 %copy-start.3 = (s32[1,32]{1,0:T(1,128)S(1)}, s32[1,32]{1,0:T(1,128)}, u32[]{:S(2)}) copy-start(s32[1,32]{1,0:T(1,128)} %param.15) | copy-start | bytes 388
  89.8 5.6 %copy-start.4 = (s32[1,16]{1,0:T(1,128)S(1)}, s32[1,16]{1,0:T(1,128)}, u32[]{:S(2)}) copy-start(s32[1,16]{1,0:T(1,128)} %param.14) | copy-start | bytes 196
  95.5 40.5 %copy-start.2 = (s32[2048]{0:T(1024)}, s32[2048]{0:T(1024)S(1)}, u32[]{:S(2)}) copy-start(s32[2048]{0:T(1024)S(1)} %select_reduce_fusion.1) | copy-start | bytes 24580
Sparse Core Ops, SparseCore 0:
  36.2 53.4 all-gather.5
  95.3 40.5 all-gather.3

commit v10 on v9

--- a/solution.py
+++ b/solution.py
@@ -75,16 +75,12 @@
 CTX = ("chip", "core")
 
 
-def gather_weights(local_w, ctx_ways):
+def gather_weights(piece, ctx_ways):
     dp_ways = lax.axis_size("dp")
-    shard_rows = local_w.shape[0]
-    piece_rows = shard_rows // ctx_ways
-    start = lax.axis_index(CTX) * piece_rows
-    piece = lax.dynamic_slice_in_dim(local_w, start, piece_rows, axis=0)
     spread = jnp.broadcast_to(piece[None], (dp_ways,) + piece.shape)
     by_shard = lax.all_to_all(spread, "dp", 0, 0, tiled=False)
     full = lax.all_gather(by_shard, CTX, axis=1, tiled=False)
-    return full.reshape(-1, local_w.shape[1])
+    return full.reshape(-1, piece.shape[1])
 
 
 def scatter_sum(terms, tok_rows):
@@ -108,11 +104,14 @@
     as_float = embed_rows.astype(jnp.float32)
     inv_rms = lax.rsqrt(jnp.mean(as_float * as_float, axis=-1, keepdims=True) + 1e-05)
     normed = (as_float * inv_rms * norm_gain).astype(jnp.bfloat16)
-    shard_rows = w_key.shape[0]
+    piece_rows = w_key.shape[0] // ctx_ways
+    start = (lax.axis_index("chip") * lax.axis_size("core") + lax.axis_index("core")) * piece_rows
+    key_piece = lax.dynamic_slice_in_dim(w_key, start, piece_rows, axis=0)
+    value_piece = lax.dynamic_slice_in_dim(w_value, start, piece_rows, axis=0)
     local_w = jnp.stack(
-        [w_key.reshape(shard_rows, KV_HEADS, HEAD), w_value.reshape(shard_rows, KV_HEADS, HEAD)],
+        [key_piece.reshape(piece_rows, KV_HEADS, HEAD), value_piece.reshape(piece_rows, KV_HEADS, HEAD)],
         axis=2,
-    ).reshape(shard_rows, 2 * KV_HEADS * HEAD)
+    ).reshape(piece_rows, 2 * KV_HEADS * HEAD)
     weights = gather_weights(local_w, ctx_ways)
     local_kv = jnp.dot(normed, weights, preferred_element_type=jnp.float32).astype(jnp.bfloat16)
     all_kv = lax.all_gather(local_kv, CTX, axis=0, tiled=True)

time: 243 us -> 241 us (level)
  no operation moved by 1% of the time
where the time goes in v10:
time: 241 us
  waiting for transfers between devices  91.6 us (38%)
  blocking collectives  65.7 us (27%)
  Pallas kernels  45 us (19%)
  between operations  13.5 us (6%)
  matrix products  11.8 us (5%)
  other arithmetic  8.25 us (3%)
  local copies, waits for them, and re-layouts  5.14 us (2%)
    all_gather x1, waiting for transfers between devices, gather_weights(): full = lax.all_gather(by_shard, CTX, axis=1, tiled=False)  53.3 us
    pallas_call x1, Pallas kernels, attend_all(): pl.pallas_call(kern, grid=(kv_heads,), in_specs=[pl.BlockSpec((tok_rows,...  45 us
    all_gather x1, waiting for transfers between devices, body(): all_kv = lax.all_gather(local_kv, CTX, axis=0, tiled=True)  38.3 us
    all_to_all x1, blocking collectives, scatter_sum(): mine = lax.all_to_all(mine, 'chip', 0, 0, tiled=False)  30.5 us
    all_to_all x1, blocking collectives, gather_weights(): by_shard = lax.all_to_all(spread, 'dp', 0, 0, tiled=False)  26.9 us
    all_to_all x1, blocking collectives, scatter_sum(): lax.all_to_all(terms.reshape(chip_ways, core_ways, tok_rows, width), 'cor...  8.19 us
    dot_general x1, matrix products, body(): lax.dot_general(own_sum, weights, contract, preferred_element_type=jnp.fl...  6.36 us
    dot_general x1, matrix products, body(): jnp.dot(normed, weights, preferred_element_type=jnp.float32)  5.42 us
  transfers between devices with their start and end apart: 2, of which 2 were waited for; matrix products, arithmetic and copies ran while one was open for 1% of the time, Pallas kernels for 0%

profile of v10, /device:TPU:1, one launch (start us, length us, event | category | flops | bytes accessed | tf_op | source)
XLA Modules:
  0.0 241.0 jit_solution(8998305922980103989)
XLA Ops:
  6.5 0.0 copy-start
  6.5 0.0 all-gather.6.cloned.1.call-start
  6.5 0.8 constant_dynamic-slice_fusion
  7.5 0.1 broadcast_in_dim.58
  7.6 26.9 %all_to_all.15 = bf16[16,16,1024]{2,1,0:T(8,128)(2,1)} all-to-all(bf16[16,16,1024]{2,1,0:T(8,128)(2,1)S(1)} %broadcast_in_dim.58), channel_id=1, replica_groups=mesh['dp'=16,'chip'=8,'core'=2] {'dp'}, dimensions={0} | all-to-all | bytes 1048576 | tf_op jit(solution)/shard_map/all_to_all | solution.py:81
  34.5 0.0 all-gather.6.cloned.1.call-update
  34.5 0.0 all-gather.4.cloned.1.call-start
  34.6 0.0 copy-done
  34.6 0.3 fusion.3
  34.9 53.3 %all-gather.6.cloned.1.call-done = bf16[16,256,1024]{2,1,0:T(8,128)(2,1)} async-done(((bf16[16,16,1024]{2,1,0:T(8,128)(2,1)}), bf16[16,256,1024]{2,1,0:T(8,128)(2,1)}) %all-gather.6.cloned.1.call-update) | async-done | bytes 8388624 | tf_op jit(solution)/shard_map/all_gather | solution.py:82
  88.2 0.0 copy-done.1
  88.2 5.4 %convolution_convert_fusion = bf16[128,1024]{1,0:T(8,128)(2,1)} fusion(bf16[4096,1024]{1,0:T(8,128)(2,1)} %bitcast.47, bf16[1,128,4096]{2,1,0:T(8,128)(2,1)S(1)} %copy-done, f32[4096]{0:T(1024)S(1)} %copy-done.1, f32[128]{0:T(128)S(1)} %add_rsqrt_fusion), kind=kOutput, calls=%fused_computation.15 | convolution fusion | flops 1075970048 | bytes 9716224 | tf_op jit(solution)/shard_map/dot_general | solution.py:116
  93.6 0.0 all-gather.4.cloned.1.call-update
  93.6 0.0 copy-done.3
  93.6 0.1 select_reduce_fusion
  93.8 0.0 copy-done.4
  93.8 0.1 select_reduce_fusion.1
  93.9 0.0 copy-start.2
  93.9 0.1 dynamic-slice_bitcast_fusion
  94.0 0.7 copy.22.qdoc_ref
  94.7 0.7 copy.21.qpos_ref
  95.4 0.6 fusion.24.kpos_ref
  96.1 38.3 %all-gather.4.cloned.1.call-done.k_ref.v_ref = bf16[2048,1024]{1,0:T(8,128)(2,1)} async-done(((bf16[128,1024]{1,0:T(8,128)(2,1)}), bf16[2048,1024]{1,0:T(8,128)(2,1)}) %all-gather.4.cloned.1.call-update) | async-done | bytes 4194320 | tf_op jit(solution)/shard_map/all_gather | solution.py:117
  134.4 0.0 copy-done.2
  134.4 45.0 %shard_map.82 = bf16[2048,1024]{1,0:T(8,128)(2,1)} custom-call(bf16[128,4096]{1,0:T(8,128)(2,1)} %bitcast.49, bf16[128,4096]{1,0:T(8,128)(2,1)} %bitcast.50, bf16[2048,1024]{1,0:T(8,128)(2,1)} %all-gather.4.cloned.1.call-done.k_ref.v_ref, bf16[2048,1024]{1,0:T(8,128)(2,1)} %all-gather.4.cloned.1.call-done.k_ref.v_ref, s32[128,1]{1,0:T(8,128)} %copy.21.qpos_ref, ...), custom_call_target="tpu_custom_call" | custom-call | tf_op jit(solution)/shard_map/pallas_call | solution.py:55
  179.3 2.6 %copy.23 = bf16[8,2,128,1024]{3,2,0,1:T(8,128)(2,1)S(1)} copy(bf16[8,2,128,1024]{3,2,1,0:T(8,128)(2,1)} %bitcast.46) | data formatting | bytes 8388608 | tf_op jit(solution)/shard_map/reshape | solution.py:91
  181.9 8.2 %all_to_all.16 = bf16[8,2,128,1024]{3,2,0,1:T(8,128)(2,1)} all-to-all(bf16[8,2,128,1024]{3,2,0,1:T(8,128)(2,1)S(1)} %copy.23), channel_id=1, replica_groups=mesh['dp'=16,'chip'=8,'core'=2] {'core'}, dimensions={1} | all-to-all | bytes 8388608 | tf_op jit(solution)/shard_map/all_to_all | solution.py:90
  190.1 3.5 %reduce_sum.63 = bf16[8,128,1024]{2,1,0:T(8,128)(2,1)S(1)} reduce(bf16[8,2,128,1024]{3,2,0,1:T(8,128)(2,1)} %all_to_all.16, bf16[]{:T(256)} %constant.77.clone.1), dimensions={1}, to_apply=%region_3.4 | reduce | flops 1048576 | bytes 6291458 | tf_op jit(solution)/shard_map/reduce_sum | solution.py:93
  193.7 30.5 %all_to_all.17 = bf16[8,128,1024]{2,1,0:T(8,128)(2,1)} all-to-all(bf16[8,128,1024]{2,1,0:T(8,128)(2,1)S(1)} %reduce_sum.63), channel_id=1, replica_groups=mesh['dp'=16,'chip'=8,'core'=2] {'chip'}, dimensions={0} | all-to-all | bytes 4194304 | tf_op jit(solution)/shard_map/all_to_all | solution.py:94
  224.2 2.0 reduce_sum.64
  226.2 6.4 %fusion.10 = (f32[128]{0:T(128)S(1)}, f32[128,4096]{1,0:T(8,128)S(1)}) fusion(bf16[1,128,4096]{2,1,0:T(8,128)(2,1)S(1)} %copy-done, f32[4096]{0:T(1024)S(1)} %copy-done.1, bf16[128,1024]{1,0:T(8,128)(2,1)S(1)} %reduce_sum.64, bf16[4096,1024]{1,0:T(8,128)(2,1)} %bitcast.48), kind=kOutput, calls=%fused_computation.12 | convolution fusion | flops 1075838848 | bytes 11813376 | tf_op jit(solution)/shard_map/dot_general | solution.py:137
  232.5 1.6 fusion.15
  (12 shorter events, 0.1 us)
Async XLA Ops:
  6.5 28.0 %copy-start = (bf16[1,128,4096]{2,1,0:T(8,128)(2,1)S(1)}, bf16[1,128,4096]{2,1,0:T(8,128)(2,1)}, u32[]{:S(2)}) copy-start(bf16[1,128,4096]{2,1,0:T(8,128)(2,1)} %param.8) | copy-start | bytes 3145732
  6.5 81.6 %copy-start.1 = (f32[4096]{0:T(1024)S(1)}, f32[4096]{0:T(1024)}, u32[]{:S(2)}) copy-start(f32[4096]{0:T(1024)} %param.9) | copy-start | bytes 49156
  6.5 81.6 %all-gather.6.cloned.1.call-start = ((), (), s32[]{:S(2)}) async-start(), calls=%async_computation.4 | async-start | bytes 8912896 | tf_op jit(solution)/shard_map/all_gather | solution.py:82
  34.5 99.8 %all-gather.4.cloned.1.call-start = ((), (), s32[]{:S(2)}) async-start(), calls=%async_computation.3 | async-start | bytes 4456448 | tf_op jit(solution)/shard_map/all_gather | solution.py:117
  88.2 5.5 %copy-start.3 = (s32[1,32]{1,0:T(1,128)S(1)}, s32[1,32]{1,0:T(1,128)}, u32[]{:S(2)}) copy-start(s32[1,32]{1,0:T(1,128)} %param.15) | copy-start | bytes 388
  88.2 5.6 %copy-start.4 = (s32[1,16]{1,0:T(1,128)S(1)}, s32[1,16]{1,0:T(1,128)}, u32[]{:S(2)}) copy-start(s32[1,16]{1,0:T(1,128)} %param.14) | copy-start | bytes 196
  93.9 40.5 %copy-start.2 = (s32[2048]{0:T(1024)}, s32[2048]{0:T(1024)S(1)}, u32[]{:S(2)}) copy-start(s32[2048]{0:T(1024)S(1)} %select_reduce_fusion.1) | copy-start | bytes 24580
Sparse Core Ops, SparseCore 0:
  34.6 53.4 all-gather.5
  93.7 40.5 all-gather.3
